TPU v7x, 32 devices: a whole 2x2x4 slice. The times are simulated.
32 devices in a mesh: seq: 8 (over z, x), mp: 4 (over y, core).
Axes of the slice: x: 2, y: 2, z: 4, core: 2. Of those that a mesh axis runs over, the one named last changes fastest.
Arguments:
- branches: bfloat16 [3, 2048, 4096], P(None, 'seq', 'mp'), may hold values from -6 to 6
- short_filter: float32 [3, 4096, 3], P(None, 'mp'), may hold values from -3.5 to 3.5
- long_filter: bfloat16 [2048, 4096], P('seq', 'mp'), may hold values from -0.125 to 0.125
- skip_gain: float32 [4096], P('mp'), may hold values from 0.5 to 1.5
- out_weight: bfloat16 [4096, 8192], P('mp'), may hold values from -0.09375 to 0.09375
Outputs:
- output: bfloat16 [2048, 8192], P('seq', 'mp')
All inputs are finite; a program needn't handle non-finite values.
Results may differ from a plain program's by a relative error of at most 0.015.
Values may be sent and summed in bfloat16 or wider, within the bound.
No kernel may reach another device: no remote copies, remote signals or barrier semaphores. Data moves between devices by JAX's collectives and lax.ppermute only.
A program may use at most 128 MiB of HBM per device.

v0:
```python
import math

import jax
import jax.numpy as jnp
import numpy as np
from jax import lax
from jax.experimental import pallas as pl
from jax.experimental.pallas import tpu as pltpu
from jax.sharding import PartitionSpec as P

ROWS = 16
F32 = jnp.float32
BF16 = jnp.bfloat16


def transform_tables(length, radix):
    ids = np.arange(length)
    angle = 2.0 * math.pi * np.mod(np.outer(ids, ids), length) / length
    cosine, sine = np.cos(angle), np.sin(angle)
    matrix = np.block([[cosine, sine], [-sine, cosine]]).astype(jnp.bfloat16)
    full = length * radix
    turn = 2.0 * math.pi * np.outer(ids, np.arange(1, radix // 2 + 1)) / full
    scale = np.where(np.arange(1, radix // 2 + 1) == radix // 2, 1.0, 2.0) / full
    columns = [np.cos(turn), np.sin(turn), np.cos(turn) * scale, np.sin(turn) * scale]
    return matrix, np.concatenate(columns, axis=1).astype(np.float32)


def axpy(total, factor, value):
    if abs(factor) < 1e-9:
        return total
    if abs(factor - 1.0) < 1e-9:
        return value if total is None else total + value
    if abs(factor + 1.0) < 1e-9:
        return -value if total is None else total - value
    term = value * np.float32(factor)
    return term if total is None else total + term


def wave(step, radix):
    angle = 2.0 * math.pi * (step % radix) / radix
    return math.cos(angle), math.sin(angle)


def across_blocks(values):
    count = len(values)
    radix, half = 2 * count, count // 2
    sums = {n: values[n] + values[count - n] for n in range(1, half)}
    diffs = {n: values[n] - values[count - n] for n in range(1, half)}
    result = []
    for k in range(count + 1):
        in_cos, in_sin = (sums, diffs) if k % 2 == 0 else (diffs, sums)
        real = axpy(values[0], wave(half * k, radix)[0], values[half])
        imag = axpy(None, -wave(half * k, radix)[1], values[half])
        for n in range(1, half):
            cosine, sine = wave(n * k, radix)
            real = axpy(real, cosine, in_cos[n])
            imag = axpy(imag, -sine, in_sin[n])
        result.append((real, imag))
    return result


def back_to_blocks(first, parts):
    count = len(parts)
    radix, half = 2 * count, count // 2
    result = [None] * count
    for n in range(half + 1):
        even_cos, even_sin, odd_cos, odd_sin = first, None, None, None
        for k in range(1, count + 1):
            real, imag = parts[k - 1]
            cosine, sine = wave(n * k, radix)
            if k % 2 == 0:
                even_cos = axpy(even_cos, cosine, real)
                if imag is not None:
                    even_sin = axpy(even_sin, -sine, imag)
            else:
                odd_cos = axpy(odd_cos, cosine, real)
                odd_sin = axpy(odd_sin, -sine, imag)

        def combined(terms):
            total = None
            for sign, term in terms:
                if term is not None:
                    total = axpy(total, sign, term)
            return total

        result[n] = combined([(1, even_cos), (1, even_sin), (1, odd_cos), (1, odd_sin)])
        if 0 < n < half:
            result[count - n] = combined(
                [(1, even_cos), (-1, even_sin), (-1, odd_cos), (1, odd_sin)]
            )
    return result


def convolve_kernel(matrix, twist, gain, signals, out, waves, turned):
    blocks, length, width = out.shape
    pairs = blocks // 2

    def chunk_of(index):
        return pl.ds(pl.multiple_of(index * ROWS, ROWS), ROWS)

    def column(rows, index):
        return jnp.broadcast_to(twist[rows, index : index + 1], (ROWS, width))

    def forward(index, carry):
        rows = chunk_of(index)
        low = pl.ds(pl.multiple_of(length + index * ROWS, ROWS), ROWS)
        for side, source in enumerate((rows, low)):
            lanes = slice(side * width, (side + 1) * width)
            spectra = across_blocks([signals[b, source, :].astype(F32) for b in range(blocks)])
            waves[0, rows, lanes] = spectra[0][0].astype(BF16)
            for k in range(1, blocks + 1):
                real, imag = spectra[k]
                cosine, sine = column(rows, k - 1), column(rows, blocks + k - 1)
                if imag is None:
                    waves[k, rows, lanes] = (real * cosine).astype(BF16)
                    waves[k, low, lanes] = (-real * sine).astype(BF16)
                else:
                    waves[k, rows, lanes] = (real * cosine + imag * sine).astype(BF16)
                    waves[k, low, lanes] = (imag * cosine - real * sine).astype(BF16)
        return carry

    lax.fori_loop(0, length // ROWS, forward, 0)

    def multiplied(spectrum):
        real, imag = spectrum[:length], spectrum[length:]
        a_real, a_imag = real[:, :width], imag[:, :width]
        b_real, b_imag = real[:, width:], imag[:, width:]
        return jnp.concatenate(
            [
                (a_real * b_real - a_imag * b_imag).astype(BF16),
                (-(a_real * b_imag + a_imag * b_real)).astype(BF16),
            ],
            axis=0,
        )

    def dot(left, right):
        return jnp.dot(left, right, preferred_element_type=F32)

    base = multiplied(dot(matrix[:, :length], waves[0, :length, :]))
    turned[pairs, :length, :width] = dot(matrix[:length, :], base)

    def one_pair(pair):
        left = multiplied(dot(matrix[...], waves[2 * pair + 1]))
        right = multiplied(dot(matrix[...], waves[2 * pair + 2]))
        turned[pair] = dot(matrix[...], jnp.concatenate([left, right], axis=1))

    if pairs <= 4:
        for pair in range(pairs):
            one_pair(pair)
    else:
        lax.fori_loop(0, pairs, lambda pair, carry: (one_pair(pair), carry)[1], 0)

    full = 2 * blocks * length
    skip = jnp.broadcast_to(gain[...], (ROWS, width))

    def backward(index, carry):
        rows = chunk_of(index)
        low = pl.ds(pl.multiple_of(length + index * ROWS, ROWS), ROWS)
        parts = []
        for k in range(1, blocks + 1):
            pair, side = (k - 1) // 2, (k - 1) % 2
            lanes = slice(side * width, (side + 1) * width)
            real, minus = turned[pair, rows, lanes], turned[pair, low, lanes]
            cosine, sine = column(rows, 2 * blocks + k - 1), column(rows, 3 * blocks + k - 1)
            turned_real = real * cosine + minus * sine
            parts.append((turned_real, None if k == blocks else real * sine - minus * cosine))
        first = turned[pairs, rows, :width] * np.float32(1.0 / full)
        for b, value in enumerate(back_to_blocks(first, parts)):
            direct = skip * signals[b, rows, :].astype(F32)
            out[b, rows, :] = (value + direct).astype(BF16)
        return carry

    lax.fori_loop(0, length // ROWS, backward, 0)


def convolve(signals, gain):
    blocks, rows, width = signals.shape
    length = rows // 2
    matrix, twist = transform_tables(length, 2 * blocks)
    return pl.pallas_call(
        convolve_kernel,
        out_shape=jax.ShapeDtypeStruct((blocks, length, width), BF16),
        scratch_shapes=[
            pltpu.VMEM((blocks + 1, 2 * length, 2 * width), BF16),
            pltpu.VMEM((blocks // 2 + 1, 2 * length, 2 * width), F32),
        ],
        compiler_params=pltpu.CompilerParams(vmem_limit_bytes=24 << 20),
        name="convolve",
    )(jnp.asarray(matrix), jnp.asarray(twist), gain, signals)


VMEM = pl.BlockSpec(memory_space=pltpu.VMEM)
SMEM = pl.BlockSpec(memory_space=pltpu.SMEM)
HBM = pl.BlockSpec(memory_space=pltpu.HBM)
STRIP = 64
TILE = 512


def smoothed(block, edge, taps, lanes, padded):
    rows, tap_count = block.shape[0], taps.shape[0]
    padded[8 - edge.shape[0] : 8, :] = edge[:, lanes].astype(F32)
    for start in range(0, rows, STRIP):
        padded[8 + start : 8 + start + STRIP, :] = block[start : start + STRIP, lanes].astype(F32)
    for start in range(0, rows, STRIP):
        total = None
        for tap in range(tap_count):
            begin = 8 - tap + start
            term = padded[begin : begin + STRIP, :] * taps[tap : tap + 1, lanes]
            total = term if total is None else total + term
        yield slice(start, start + STRIP), total


def product_kernel(branches, edges, taps, filt, out, padded):
    parts, rows, width = out.shape[0], filt.shape[0], out.shape[2]
    for j in range(parts):
        lanes = slice(j * width, (j + 1) * width)
        first, third = (
            smoothed(branches.at[b], edges.at[b], taps.at[b], lanes, padded.at[j % 2, b // 2])
            for b in (0, 2)
        )
        for (span, left), (span, right) in zip(first, third):
            out[j, span, :] = (left * right).astype(BF16)
        out[j, rows:, :] = filt[:, lanes]


def product_and_filter(branches, edges, taps, filt, parts):
    rows, channels = filt.shape
    width = channels // parts
    return pl.pallas_call(
        product_kernel,
        in_specs=[VMEM] * 4,
        out_specs=VMEM,
        out_shape=jax.ShapeDtypeStruct((parts, 2 * rows, width), BF16),
        scratch_shapes=[pltpu.VMEM((2, 2, rows + 8, width), F32)],
        name="product",
    )(branches, edges, taps, filt)


def weight_copies(weight, held, sems, block):
    columns = held.shape[1]
    result = []
    for index, start in enumerate(range(0, columns, TILE)):
        span = pl.ds(pl.multiple_of(block * columns + start, TILE), TILE)
        target = held.at[:, start : start + TILE]
        result.append(pltpu.make_async_copy(weight.at[:, span], target, sems.at[index]))
    return result


def project_into(out, gated, held, copies):
    for copy, start in zip(copies, range(0, out.shape[1], TILE)):
        span = slice(start, start + TILE)
        copy.wait()
        value = jnp.dot(gated[...], held[:, span], preferred_element_type=F32)
        out[:, span] = value.astype(out.dtype)


def gate_kernel(place, mixed, branch, edges, taps, weight, gated, part, padded, held, sems):
    copies = weight_copies(weight, held, sems, place[0] ^ 3)
    for copy in copies:
        copy.start()
    parts, width = mixed.shape[0], mixed.shape[2]
    for j in range(parts):
        lanes = slice(j * width, (j + 1) * width)
        for span, second in smoothed(branch, edges.at[1], taps.at[1], lanes, padded.at[j % 2]):
            gated[span, lanes] = (second * mixed[j, span, :].astype(F32)).astype(BF16)
    project_into(part, gated, held, copies)


def rest_kernel(place, gated, weight, far_own, near_part, near_own, held, sems):
    outs = (far_own, near_part, near_own)
    sets = [
        weight_copies(weight, held.at[i], sems.at[i], place[0] ^ flip)
        for i, flip in enumerate((2, 1, 0))
    ]
    for copies in sets:
        for copy in copies:
            copy.start()
    for i, out in enumerate(outs):
        project_into(out, gated, held.at[i], sets[i])


def shards(branches, short_filter, long_filter, skip_gain, out_weight):
    seq_count, mp_count = lax.axis_size("seq"), lax.axis_size("mp")
    tokens, channels = long_filter.shape
    width = channels // seq_count
    features = out_weight.shape[1] // mp_count
    tap_count = short_filter.shape[2]
    me, place = lax.axis_index("mp"), lax.axis_index("seq")

    def exchanged(value, bit):
        return lax.ppermute(value, "mp", [(m, m ^ bit) for m in range(mp_count)])

    taps = jnp.transpose(short_filter, (0, 2, 1))
    edges = lax.ppermute(
        branches[:, tokens - (tap_count - 1) :, :],
        "seq",
        [(s, s + 1) for s in range(seq_count - 1)],
    )
    signals = product_and_filter(branches, edges, taps, long_filter, seq_count)
    signals = lax.all_to_all(signals, "seq", 0, 0, tiled=True)
    gain = lax.dynamic_slice(skip_gain, (place * width,), (width,)).reshape(1, width)
    mixed = convolve(signals, gain)
    mixed = lax.all_to_all(mixed, "seq", 0, 0, tiled=True)

    def result(dtype):
        return jax.ShapeDtypeStruct((tokens, features), dtype)

    params = pltpu.CompilerParams(vmem_limit_bytes=50 << 20)
    me = me.reshape(1)
    gated, part = pl.pallas_call(
        gate_kernel,
        in_specs=[SMEM] + [VMEM] * 4 + [HBM],
        out_specs=[VMEM] * 2,
        out_shape=[jax.ShapeDtypeStruct((tokens, channels), BF16), result(BF16)],
        scratch_shapes=[
            pltpu.VMEM((2, tokens + 8, width), F32),
            pltpu.VMEM((channels, features), BF16),
            pltpu.SemaphoreType.DMA((features // TILE,)),
        ],
        compiler_params=params,
        name="gate",
    )(me, mixed, branches[1], edges, taps, out_weight)
    other = exchanged(part, 1)
    far_own, near_part, near_own = pl.pallas_call(
        rest_kernel,
        in_specs=[SMEM, VMEM, HBM],
        out_specs=[VMEM] * 3,
        out_shape=[result(F32), result(BF16), result(F32)],
        scratch_shapes=[
            pltpu.VMEM((3, channels, features), BF16),
            pltpu.SemaphoreType.DMA((3, features // TILE)),
        ],
        compiler_params=params,
        name="rest",
    )(me, gated, out_weight)
    sent = (far_own + other.astype(F32)).astype(BF16)
    far = exchanged(sent, 2)
    near = near_own + exchanged(near_part, 1).astype(F32)
    return (near + far.astype(F32)).astype(BF16)


def solution(mesh):
    return jax.shard_map(
        shards,
        mesh=mesh,
        in_specs=(
            P(None, "seq", "mp"),
            P(None, "mp", None),
            P("seq", "mp"),
            P("mp"),
            P("mp", None),
        ),
        out_specs=P("seq", "mp"),
        check_vma=False,
    )
```

profile of v0, /device:TPU:0, one launch (start us, length us, event | category | flops | bytes accessed | tf_op | source)
XLA Modules:
  0.0 108.1 jit_solution(6752559313742104539)
XLA Ops:
  0.0 0.0 copy-start
  0.0 0.8 slice.6
  0.8 4.8 %collective-permute-start = (bf16[3,2,1024]{2,1,0:T(2,128)(2,1)S(1)}, bf16[3,2,1024]{2,1,0:T(2,128)(2,1)S(1)}, u32[]{:S(2)}, u32[]{:S(2)}) collective-permute-start(bf16[3,2,1024]{2,1,0:T(2,128)(2,1)S(1)} %slice.6), channel_id=1, source_target_pairs={{0,4},{4,8},{8,12},{12,16},{16,20},{20,24},{24,28},{1,5},{5,9},{9,... | collective-permute-start | bytes 36872 | tf_op jit(solution)/shard_map/ppermute | solution.py:294
  5.7 1.4 %collective-permute-done.edges = bf16[3,2,1024]{2,1,0:T(2,128)(2,1)S(1)} collective-permute-done((bf16[3,2,1024]{2,1,0:T(2,128)(2,1)S(1)}, bf16[3,2,1024]{2,1,0:T(2,128)(2,1)S(1)}, u32[]{:S(2)}, u32[]{:S(2)}) %collective-permute-start) | collective-permute-done | bytes 12320 | tf_op jit(solution)/shard_map/ppermute | solution.py:294
  7.1 0.0 copy-start.4
  7.1 0.6 copy-done.4
  7.7 0.0 copy-start.1
  7.7 0.0 copy-start.3
  7.7 3.3 %product.1 = bf16[8,512,128]{2,1,0:T(8,128)(2,1)} custom-call(bf16[3,256,1024]{2,1,0:T(8,128)(2,1)} %branches.1, bf16[3,2,1024]{2,1,0:T(2,128)(2,1)} %copy-done.4, f32[3,3,1024]{2,1,0:T(4,128)} %bitcast.6, bf16[256,1024]{1,0:T(8,128)(2,1)} %filt.1), custom_call_target="tpu_custom_call" | custom-call | tf_op jit(solution)/shard_map/product/pallas_call | solution.py:229
  10.9 6.6 %all-to-all-start = ((bf16[8,512,128]{2,1,0:T(8,128)(2,1)}), bf16[8,512,128]{2,1,0:T(8,128)(2,1)S(1)}, u32[]{:S(2)}, u32[]{:S(2)}) async-start(bf16[8,512,128]{2,1,0:T(8,128)(2,1)} %product.1), calls=%async_computation | async-start | bytes 2097152 | tf_op jit(solution)/shard_map/all_to_all | solution.py:300
  17.5 0.0 copy-done
  17.6 0.1 dynamic-slice_bitcast_fusion.gain
  17.6 0.0 copy-start.2
  17.6 0.0 copy-start.5
  17.6 24.8 %all-to-all-done.signals = bf16[8,512,128]{2,1,0:T(8,128)(2,1)S(1)} async-done(((bf16[8,512,128]{2,1,0:T(8,128)(2,1)}), bf16[8,512,128]{2,1,0:T(8,128)(2,1)S(1)}, u32[]{:S(2)}, u32[]{:S(2)}) %all-to-all-start) | async-done | bytes 1048608 | tf_op jit(solution)/shard_map/all_to_all | solution.py:300
  42.4 0.0 copy-done.1
  42.4 0.0 copy-done.3
  42.4 9.0 %convolve.1 = bf16[8,256,128]{2,1,0:T(8,128)(2,1)} custom-call(bf16[512,512]{1,0:T(8,128)(2,1)S(1)} %copy-done.1, f32[256,32]{1,0:T(8,128)S(1)} %copy-done.3, f32[1,128]{1,0:T(1,128)S(1)} %dynamic-slice_bitcast_fusion.gain, bf16[8,512,128]{2,1,0:T(8,128)(2,1)S(1)} %all-to-all-done.signals), custom_call_target="tpu_custom_call" | custom-call | tf_op jit(solution)/shard_map/convolve/pallas_call | solution.py:180
  51.4 3.5 %all-to-all-start.1 = ((bf16[8,256,128]{2,1,0:T(8,128)(2,1)}), bf16[8,256,128]{2,1,0:T(8,128)(2,1)S(1)}, u32[]{:S(2)}, u32[]{:S(2)}) async-start(bf16[8,256,128]{2,1,0:T(8,128)(2,1)} %convolve.1), calls=%async_computation.1 | async-start | bytes 1048576 | tf_op jit(solution)/shard_map/all_to_all | solution.py:303
  54.9 1.1 slice_bitcast_fusion.branch
  55.9 13.5 %all-to-all-done.1.mixed = bf16[8,256,128]{2,1,0:T(8,128)(2,1)S(1)} async-done(((bf16[8,256,128]{2,1,0:T(8,128)(2,1)}), bf16[8,256,128]{2,1,0:T(8,128)(2,1)S(1)}, u32[]{:S(2)}, u32[]{:S(2)}) %all-to-all-start.1) | async-done | bytes 524320 | tf_op jit(solution)/shard_map/all_to_all | solution.py:303
  69.4 0.0 copy-done.2
  69.4 0.0 copy-done.5
  69.4 3.1 %gate.1 = (bf16[256,1024]{1,0:T(8,128)(2,1)S(1)}, bf16[256,2048]{1,0:T(8,128)(2,1)S(1)}) custom-call(s32[1]{0:T(128)} %bitcast.place, bf16[8,256,128]{2,1,0:T(8,128)(2,1)S(1)} %all-to-all-done.1.mixed, bf16[256,1024]{1,0:T(8,128)(2,1)S(1)} %slice_bitcast_fusion.branch, bf16[3,2,1024]{2,1,0:T(2,128)(2,1)S(1)} %copy-done.5, f32[3,3,1024]{2,1,0:T(4,128)S(1)} %bitcast.7, ...), custom_call_target="tpu_custom_call" | custom-call | tf_op jit(solution)/shard_map/gate/pallas_call | solution.py:310
  72.5 0.1 collective-permute-start.2
  72.6 8.0 %rest.1 = (f32[256,2048]{1,0:T(8,128)S(1)}, bf16[256,2048]{1,0:T(8,128)(2,1)S(1)}, f32[256,2048]{1,0:T(8,128)}) custom-call(s32[1]{0:T(128)} %bitcast.place, bf16[256,1024]{1,0:T(8,128)(2,1)S(1)} %get-tuple-element.10.gated, bf16[1024,8192]{1,0:T(8,128)(2,1)} %weight.3), custom_call_target="tpu_custom_call" | custom-call | tf_op jit(solution)/shard_map/rest/pallas_call | solution.py:324
  80.6 0.6 collective-permute-start.1
  81.2 0.0 collective-permute-done.2
  81.2 0.0 copy-start.6
  81.2 0.3 add_convert_fusion.1
  81.5 1.6 %collective-permute-start.3 = (bf16[256,2048]{1,0:T(8,128)(2,1)S(1)}, bf16[256,2048]{1,0:T(8,128)(2,1)S(1)}, u32[]{:S(2)}, u32[]{:S(2)}) collective-permute-start(bf16[256,2048]{1,0:T(8,128)(2,1)S(1)} %add_convert_fusion.1), channel_id=1, source_target_pairs={{0,2},{1,3},{2,0},{3,1},{4,6},{5,7},{6,4},{7,5},{8,10},{9,11},{10,... | collective-permute-start | bytes 3145736 | tf_op jit(solution)/shard_map/ppermute | solution.py:291
  83.1 0.4 collective-permute-done.1
  83.5 23.2 %collective-permute-done.3 = bf16[256,2048]{1,0:T(8,128)(2,1)S(1)} collective-permute-done((bf16[256,2048]{1,0:T(8,128)(2,1)S(1)}, bf16[256,2048]{1,0:T(8,128)(2,1)S(1)}, u32[]{:S(2)}, u32[]{:S(2)}) %collective-permute-start.3) | collective-permute-done | bytes 1048608 | tf_op jit(solution)/shard_map/ppermute | solution.py:291
  106.7 0.0 copy-done.6
  106.7 1.4 %add_convert_fusion = bf16[256,2048]{1,0:T(8,128)(2,1)} fusion(bf16[256,2048]{1,0:T(8,128)(2,1)S(1)} %collective-permute-done.3, f32[256,2048]{1,0:T(8,128)S(1)} %copy-done.6, bf16[256,2048]{1,0:T(8,128)(2,1)S(1)} %collective-permute-done.1), kind=kLoop, calls=%fused_computation | loop fusion | flops 2621440 | bytes 5242880 | tf_op jit(solution)/shard_map/convert_element_type | solution.py:339
Async XLA Ops:
  0.0 17.5 %copy-start = (f32[1024]{0:T(1024)S(1)}, f32[1024]{0:T(1024)}, u32[]{:S(2)}) copy-start(f32[1024]{0:T(1024)} %param.10) | copy-start | bytes 12292
  0.8 6.2 %collective-permute-start = (bf16[3,2,1024]{2,1,0:T(2,128)(2,1)S(1)}, bf16[3,2,1024]{2,1,0:T(2,128)(2,1)S(1)}, u32[]{:S(2)}, u32[]{:S(2)}) collective-permute-start(bf16[3,2,1024]{2,1,0:T(2,128)(2,1)S(1)} %slice.6), channel_id=1, source_target_pairs={{0,4},{4,8},{8,12},{12,16},{16,20},{20,24},{24,28},{1,5},{5,9},{9,... | collective-permute-start | bytes 36872 | tf_op jit(solution)/shard_map/ppermute | solution.py:294
  7.1 0.6 copy-start.4
  7.7 34.7 %copy-start.1 = (bf16[512,512]{1,0:T(8,128)(2,1)S(1)}, bf16[512,512]{1,0:T(8,128)(2,1)}, u32[]{:S(2)}) copy-start(bf16[512,512]{1,0:T(8,128)(2,1)} %constant.19.clone.matrix) | copy-start | bytes 1572868
  7.7 34.7 %copy-start.3 = (f32[256,32]{1,0:T(8,128)S(1)}, f32[256,32]{1,0:T(8,128)}, u32[]{:S(2)}) copy-start(f32[256,32]{1,0:T(8,128)} %constant.20.clone.twist) | copy-start | bytes 98308
  10.9 31.4 %all-to-all-start = ((bf16[8,512,128]{2,1,0:T(8,128)(2,1)}), bf16[8,512,128]{2,1,0:T(8,128)(2,1)S(1)}, u32[]{:S(2)}, u32[]{:S(2)}) async-start(bf16[8,512,128]{2,1,0:T(8,128)(2,1)} %product.1), calls=%async_computation | async-start | bytes 2097152 | tf_op jit(solution)/shard_map/all_to_all | solution.py:300
  17.6 51.8 %copy-start.2 = (f32[3,1024,3]{1,2,0:T(4,128)S(1)}, f32[3,1024,3]{1,2,0:T(4,128)}, u32[]{:S(2)}) copy-start(f32[3,1024,3]{1,2,0:T(4,128)} %param.8) | copy-start | bytes 110596
  17.6 51.8 %copy-start.5 = (bf16[3,2,1024]{2,1,0:T(2,128)(2,1)S(1)}, bf16[3,2,1024]{2,1,0:T(2,128)(2,1)}, u32[]{:S(2)}) copy-start(bf16[3,2,1024]{2,1,0:T(2,128)(2,1)} %copy-done.4) | copy-start | bytes 36868
  51.4 18.1 %all-to-all-start.1 = ((bf16[8,256,128]{2,1,0:T(8,128)(2,1)}), bf16[8,256,128]{2,1,0:T(8,128)(2,1)S(1)}, u32[]{:S(2)}, u32[]{:S(2)}) async-start(bf16[8,256,128]{2,1,0:T(8,128)(2,1)} %convolve.1), calls=%async_computation.1 | async-start | bytes 1048576 | tf_op jit(solution)/shard_map/all_to_all | solution.py:303
  72.5 8.7 %collective-permute-start.2 = (bf16[256,2048]{1,0:T(8,128)(2,1)S(1)}, bf16[256,2048]{1,0:T(8,128)(2,1)S(1)}, u32[]{:S(2)}, u32[]{:S(2)}) collective-permute-start(bf16[256,2048]{1,0:T(8,128)(2,1)S(1)} %get-tuple-element.14), channel_id=1, source_target_pairs={{0,1},{1,0},{2,3},{3,2},{4,5},{5,4},{6,7},{7,6},{8,9},{9,8},{10,11... | collective-permute-start | bytes 3145736 | tf_op jit(solution)/shard_map/ppermute | solution.py:291
  80.6 2.8 %collective-permute-start.1 = (bf16[256,2048]{1,0:T(8,128)(2,1)S(1)}, bf16[256,2048]{1,0:T(8,128)(2,1)S(1)}, u32[]{:S(2)}, u32[]{:S(2)}) collective-permute-start(bf16[256,2048]{1,0:T(8,128)(2,1)S(1)} %get-tuple-element.12), channel_id=1, source_target_pairs={{0,1},{1,0},{2,3},{3,2},{4,5},{5,4},{6,7},{7,6},{8,9},{9,8},{10,11... | collective-permute-start | bytes 3145736 | tf_op jit(solution)/shard_map/ppermute | solution.py:291
  81.2 25.5 %copy-start.6 = (f32[256,2048]{1,0:T(8,128)S(1)}, f32[256,2048]{1,0:T(8,128)}, u32[]{:S(2)}) copy-start(f32[256,2048]{1,0:T(8,128)} %get-tuple-element.11) | copy-start | bytes 6291460
  81.5 25.2 %collective-permute-start.3 = (bf16[256,2048]{1,0:T(8,128)(2,1)S(1)}, bf16[256,2048]{1,0:T(8,128)(2,1)S(1)}, u32[]{:S(2)}, u32[]{:S(2)}) collective-permute-start(bf16[256,2048]{1,0:T(8,128)(2,1)S(1)} %add_convert_fusion.1), channel_id=1, source_target_pairs={{0,2},{1,3},{2,0},{3,1},{4,6},{5,7},{6,4},{7,5},{8,10},{9,11},{10,... | collective-permute-start | bytes 3145736 | tf_op jit(solution)/shard_map/ppermute | solution.py:291
where the time goes:
time: 109 us; the launch traced here: 108 us
  waiting for transfers between devices  63.2 us (58%)
  Pallas kernels  23.3 us (21%)
  starting transfers between devices  17.2 us (16%)
  local copies, waits for them, and re-layouts  2.6 us (2%)
  other arithmetic  1.77 us (2%)
    all_to_all x1, waiting for transfers between devices, shards(): signals = lax.all_to_all(signals, 'seq', 0, 0, tiled=True)  24.8 us
    ppermute x3, waiting for transfers between devices, exchanged(): return lax.ppermute(value, 'mp', [(m, m ^ bit) for m in range(mp_count)])  23.6 us
    all_to_all x1, waiting for transfers between devices, shards(): mixed = lax.all_to_all(mixed, 'seq', 0, 0, tiled=True)  13.5 us
    pallas_call x1, Pallas kernels, convolve(): pl.pallas_call(convolve_kernel, out_shape=jax.ShapeDtypeStruct((blocks, l...  8.97 us
    pallas_call x1, Pallas kernels, shards(): pl.pallas_call(rest_kernel, in_specs=[SMEM, VMEM, HBM], out_specs=[VMEM]...  8.03 us
    all_to_all x1, starting transfers between devices, shards(): signals = lax.all_to_all(signals, 'seq', 0, 0, tiled=True)  6.6 us
    ppermute x1, starting transfers between devices, shards(): lax.ppermute(branches[:, tokens - (tap_count - 1):, :], 'seq', [(s, s + 1...  4.84 us
    all_to_all x1, starting transfers between devices, shards(): mixed = lax.all_to_all(mixed, 'seq', 0, 0, tiled=True)  3.49 us
  transfers between devices with their start and end apart: 6, of which 5 were waited for; matrix products, arithmetic and copies ran while one was open for 1% of the time, Pallas kernels for 7%

commit v1 on v0

v1 whole, which is shorter than its diff:
```python
import functools
import math

import jax
import jax.numpy as jnp
import numpy as np
from jax import lax
from jax.experimental import pallas as pl
from jax.experimental.pallas import tpu as pltpu
from jax.sharding import PartitionSpec as P

ROWS = 16
F32 = jnp.float32
BF16 = jnp.bfloat16


def transform_tables(length, radix):
    ids = np.arange(length)
    angle = 2.0 * math.pi * np.mod(np.outer(ids, ids), length) / length
    cosine, sine = np.cos(angle), np.sin(angle)
    matrix = np.block([[cosine, sine], [-sine, cosine]]).astype(jnp.bfloat16)
    full = length * radix
    turn = 2.0 * math.pi * np.outer(ids, np.arange(1, radix // 2 + 1)) / full
    scale = np.where(np.arange(1, radix // 2 + 1) == radix // 2, 1.0, 2.0) / full
    columns = [np.cos(turn), np.sin(turn), np.cos(turn) * scale, np.sin(turn) * scale]
    return matrix, np.concatenate(columns, axis=1).astype(np.float32)


def axpy(total, factor, value):
    if abs(factor) < 1e-9:
        return total
    if abs(factor - 1.0) < 1e-9:
        return value if total is None else total + value
    if abs(factor + 1.0) < 1e-9:
        return -value if total is None else total - value
    term = value * np.float32(factor)
    return term if total is None else total + term


def wave(step, radix):
    angle = 2.0 * math.pi * (step % radix) / radix
    return math.cos(angle), math.sin(angle)


def across_blocks(values):
    count = len(values)
    radix, half = 2 * count, count // 2
    sums = {n: values[n] + values[count - n] for n in range(1, half)}
    diffs = {n: values[n] - values[count - n] for n in range(1, half)}
    result = []
    for k in range(count + 1):
        in_cos, in_sin = (sums, diffs) if k % 2 == 0 else (diffs, sums)
        real = axpy(values[0], wave(half * k, radix)[0], values[half])
        imag = axpy(None, -wave(half * k, radix)[1], values[half])
        for n in range(1, half):
            cosine, sine = wave(n * k, radix)
            real = axpy(real, cosine, in_cos[n])
            imag = axpy(imag, -sine, in_sin[n])
        result.append((real, imag))
    return result


def back_to_blocks(first, parts):
    count = len(parts)
    radix, half = 2 * count, count // 2
    result = [None] * count
    for n in range(half + 1):
        even_cos, even_sin, odd_cos, odd_sin = first, None, None, None
        for k in range(1, count + 1):
            real, imag = parts[k - 1]
            cosine, sine = wave(n * k, radix)
            if k % 2 == 0:
                even_cos = axpy(even_cos, cosine, real)
                if imag is not None:
                    even_sin = axpy(even_sin, -sine, imag)
            else:
                odd_cos = axpy(odd_cos, cosine, real)
                odd_sin = axpy(odd_sin, -sine, imag)

        def combined(terms):
            total = None
            for sign, term in terms:
                if term is not None:
                    total = axpy(total, sign, term)
            return total

        result[n] = combined([(1, even_cos), (1, even_sin), (1, odd_cos), (1, odd_sin)])
        if 0 < n < half:
            result[count - n] = combined(
                [(1, even_cos), (-1, even_sin), (-1, odd_cos), (1, odd_sin)]
            )
    return result


VMEM = pl.BlockSpec(memory_space=pltpu.VMEM)
SMEM = pl.BlockSpec(memory_space=pltpu.SMEM)
HBM = pl.BlockSpec(memory_space=pltpu.HBM)
STRIP = 64
TILE = 512
BRANCHES = 3


def cost(flops, moved):
    return pl.CostEstimate(flops=int(flops), bytes_accessed=int(moved), transcendentals=0)


def smoothed(block, taps, lanes, padded, start, rows):
    if start == 0:
        padded[:ROWS, :] = jnp.zeros((ROWS, padded.shape[1]), F32)
    else:
        padded[:ROWS, :] = block[start - ROWS : start, lanes].astype(F32)
    strip = min(STRIP, rows)
    for begin in range(0, rows, strip):
        value = block[start + begin : start + begin + strip, lanes].astype(F32)
        padded[ROWS + begin : ROWS + begin + strip, :] = value
    for begin in range(0, rows, strip):
        total = None
        for tap in range(taps.shape[0]):
            first = ROWS - tap + begin
            term = padded[first : first + strip, :] * taps[tap : tap + 1, lanes]
            total = term if total is None else total + term
        yield slice(begin, begin + strip), total


def product_kernel(branches, taps, filt, out, padded):
    parts, width = out.shape[0], out.shape[2]
    rows, edge = filt.shape[0], taps.shape[1] - 1
    for j in range(parts):
        lanes = slice(j * width, (j + 1) * width)
        first, third = (
            smoothed(branches.at[b], taps.at[b], lanes, padded.at[j % 2, b // 2], 0, rows)
            for b in (0, 2)
        )
        for (span, left), (span, right) in zip(first, third):
            out[j, span, :] = (left * right).astype(BF16)
        out[j, rows : 2 * rows, :] = filt[:, lanes]
        rims = [branches[b, rows - ROWS :, lanes].astype(F32)[-edge:] for b in range(BRANCHES)]
        rims += [branches[b, :ROWS, lanes].astype(F32)[:edge] for b in range(BRANCHES)]
        unused = out.shape[1] - 2 * rows - 2 * BRANCHES * edge
        if unused:
            rims.append(jnp.zeros((unused, width), F32))
        out[j, 2 * rows :, :] = jnp.concatenate(rims, axis=0).astype(BF16)


def signals_of(branches, taps, filt, parts):
    rows, channels = filt.shape
    width = channels // parts
    rims = -(-2 * BRANCHES * (taps.shape[1] - 1) // ROWS) * ROWS
    return pl.pallas_call(
        product_kernel,
        in_specs=[VMEM] * 3,
        out_specs=VMEM,
        out_shape=jax.ShapeDtypeStruct((parts, 2 * rows + rims, width), BF16),
        scratch_shapes=[pltpu.VMEM((2, 2, rows + ROWS, width), F32)],
        cost_estimate=cost(40 * rows * channels, 10 * rows * channels),
        name="product",
    )(branches, taps, filt)


def chunk_of(index, offset=0):
    return pl.ds(pl.multiple_of(offset + index * ROWS, ROWS), ROWS)


def column(twist, rows, index, width):
    return jnp.broadcast_to(twist[rows, index : index + 1], (ROWS, width))


def first_rows(signals, taps, length):
    edge = taps.shape[1] - 1
    rims = signals[:, 2 * length :, :].astype(F32)
    result = []
    for branch in range(BRANCHES):
        before, after = (
            [rims[:, (side * BRANCHES + branch) * edge + i, :] for i in range(edge)]
            for side in (0, 1)
        )
        zero = jnp.zeros_like(before[0][:1])
        rows = [jnp.concatenate([zero, row[:-1]], axis=0) for row in before] + after
        smooth = []
        for i in range(edge):
            total = None
            for tap in range(edge + 1):
                term = rows[edge + i - tap] * taps[branch, tap : tap + 1, :]
                total = term if total is None else total + term
            smooth.append(total)
        result.append(smooth)
    return result


def replaced(tile, rows):
    ids = lax.broadcasted_iota(jnp.int32, tile.shape, 0)
    for i, row in enumerate(rows):
        tile = jnp.where(ids == i, jnp.broadcast_to(row, tile.shape), tile)
    return tile


def transform_kernel(matrix, twist, taps, signals, turned, product, gates, waves):
    blocks, length, width = product.shape
    pairs = blocks // 2

    smooth = first_rows(signals, taps, length)
    for b in range(blocks):
        product[b, ROWS:, :] = signals[b, ROWS:length, :]
        heads = [smooth[0][i][b : b + 1] * smooth[2][i][b : b + 1] for i in range(len(smooth[0]))]
        product[b, :ROWS, :] = replaced(signals[b, :ROWS, :].astype(F32), heads).astype(BF16)
        gains = [smooth[1][i][b : b + 1] for i in range(len(smooth[1]))]
        gates[b] = replaced(jnp.ones((ROWS, width), F32), gains)

    def forward(index, carry):
        rows, low = chunk_of(index), chunk_of(index, length)
        for side in (0, 1):
            lanes = slice(side * width, (side + 1) * width)
            if side == 0:
                values = [product[b, rows, :].astype(F32) for b in range(blocks)]
            else:
                values = [signals[b, low, :].astype(F32) for b in range(blocks)]
            spectra = across_blocks(values)
            waves[0, rows, lanes] = spectra[0][0].astype(BF16)
            for k in range(1, blocks + 1):
                real, imag = spectra[k]
                cosine = column(twist, rows, k - 1, width)
                sine = column(twist, rows, blocks + k - 1, width)
                if imag is None:
                    waves[k, rows, lanes] = (real * cosine).astype(BF16)
                    waves[k, low, lanes] = (-real * sine).astype(BF16)
                else:
                    waves[k, rows, lanes] = (real * cosine + imag * sine).astype(BF16)
                    waves[k, low, lanes] = (imag * cosine - real * sine).astype(BF16)
        return carry

    lax.fori_loop(0, length // ROWS, forward, 0)

    def multiplied(spectrum):
        real, imag = spectrum[:length], spectrum[length:]
        a_real, a_imag = real[:, :width], imag[:, :width]
        b_real, b_imag = real[:, width:], imag[:, width:]
        return jnp.concatenate(
            [
                (a_real * b_real - a_imag * b_imag).astype(BF16),
                (-(a_real * b_imag + a_imag * b_real)).astype(BF16),
            ],
            axis=0,
        )

    def dot(left, right):
        return jnp.dot(left, right, preferred_element_type=F32)

    base = multiplied(dot(matrix[:, :length], waves[0, :length, :]))
    turned[pairs, :length, :width] = dot(matrix[:length, :], base)

    def one_pair(pair):
        left = multiplied(dot(matrix[...], waves[2 * pair + 1]))
        right = multiplied(dot(matrix[...], waves[2 * pair + 2]))
        turned[pair] = dot(matrix[...], jnp.concatenate([left, right], axis=1))

    if pairs <= 4:
        for pair in range(pairs):
            one_pair(pair)
    else:
        lax.fori_loop(0, pairs, lambda pair, carry: (one_pair(pair), carry)[1], 0)


def back_kernel(start, twist, gain, gates, turned, product, out):
    blocks, count, width = out.shape
    length = product.shape[1]
    full, pairs = 2 * blocks * length, blocks // 2
    skip = jnp.broadcast_to(gain[...], (ROWS, width))

    def backward(index, carry):
        rows, low = chunk_of(index, start), chunk_of(index, length + start)
        parts = []
        for k in range(1, blocks + 1):
            pair, side = (k - 1) // 2, (k - 1) % 2
            lanes = slice(side * width, (side + 1) * width)
            real, minus = turned[pair, rows, lanes], turned[pair, low, lanes]
            cosine = column(twist, rows, 2 * blocks + k - 1, width)
            sine = column(twist, rows, 3 * blocks + k - 1, width)
            turned_real = real * cosine + minus * sine
            parts.append((turned_real, None if k == blocks else real * sine - minus * cosine))
        first = turned[pairs, rows, :width] * np.float32(1.0 / full)
        for b, value in enumerate(back_to_blocks(first, parts)):
            direct = skip * product[b, rows, :].astype(F32)
            out[b, chunk_of(index), :] = (value + direct).astype(BF16)
        return carry

    lax.fori_loop(0, count // ROWS, backward, 0)
    if start == 0:
        for b in range(blocks):
            out[b, :ROWS, :] = (out[b, :ROWS, :].astype(F32) * gates[b]).astype(BF16)


def weight_copies(weight, held, sems, block):
    columns = held.shape[1]
    result = []
    for index, start in enumerate(range(0, columns, TILE)):
        span = pl.ds(pl.multiple_of(block * columns + start, TILE), TILE)
        target = held.at[:, start : start + TILE]
        result.append(pltpu.make_async_copy(weight.at[:, span], target, sems.at[index]))
    return result


def project_into(out, gated, held, copies):
    for copy, start in zip(copies, range(0, out.shape[1], TILE)):
        span = slice(start, start + TILE)
        copy.wait()
        value = jnp.dot(gated, held[:, span], preferred_element_type=F32)
        out[:, span] = value.astype(out.dtype)


def gate_kernel(start, place, mixed, branch, taps, weight, gated, part, padded, held, sems):
    copies = weight_copies(weight, held, sems, place[0] ^ 3)
    for copy in copies:
        copy.start()
    parts, rows, width = mixed.shape
    for j in range(parts):
        lanes = slice(j * width, (j + 1) * width)
        strips = smoothed(branch, taps.at[1], lanes, padded.at[j % 2], start, rows)
        for span, second in strips:
            value = mixed[j, span, :].astype(F32)
            done = second * value
            if start == 0 and span.start == 0:
                ids = lax.broadcasted_iota(jnp.int32, done.shape, 0)
                done = jnp.where(ids < taps.shape[1] - 1, value, done)
            gated[span, lanes] = done.astype(BF16)
    project_into(part, gated[...], held, copies)


def own_kernel(place, gated, weight, own, held, sems):
    copies = weight_copies(weight, held, sems, place[0] ^ 2)
    for copy in copies:
        copy.start()
    project_into(own, gated[...], held, copies)


def near_kernel(place, gated, weight, part, own, held, sems):
    sets = [weight_copies(weight, held.at[i], sems.at[i], place[0] ^ (1 - i)) for i in (0, 1)]
    for copies in sets:
        for copy in copies:
            copy.start()
    for i, out in enumerate((part, own)):
        project_into(out, gated[...], held.at[i], sets[i])


def shards(branches, short_filter, long_filter, skip_gain, out_weight):
    seq_count, mp_count = lax.axis_size("seq"), lax.axis_size("mp")
    tokens, channels = long_filter.shape
    width = channels // seq_count
    features = out_weight.shape[1] // mp_count
    me, place = lax.axis_index("mp").reshape(1), lax.axis_index("seq")
    params = pltpu.CompilerParams(vmem_limit_bytes=50 << 20)
    small = pltpu.CompilerParams(vmem_limit_bytes=24 << 20)
    half = tokens
    starts = (0,)

    def exchanged(value, bit):
        return lax.ppermute(value, "mp", [(m, m ^ bit) for m in range(mp_count)])

    def across(value):
        return lax.all_to_all(value, "seq", 0, 0, tiled=True)

    def shape(rows, dtype):
        return jax.ShapeDtypeStruct((rows, features), dtype)

    taps = jnp.transpose(short_filter, (0, 2, 1))
    signals = across(signals_of(branches, taps, long_filter, seq_count))

    mine = place * width
    gain = lax.dynamic_slice(skip_gain, (mine,), (width,)).reshape(1, width)
    my_taps = lax.dynamic_slice_in_dim(taps, mine, width, 2)
    matrix, twist = (jnp.asarray(t) for t in transform_tables(tokens, 2 * seq_count))
    turned, product, gates = pl.pallas_call(
        transform_kernel,
        in_specs=[VMEM] * 4,
        out_specs=[VMEM] * 3,
        out_shape=[
            jax.ShapeDtypeStruct((seq_count // 2 + 1, 2 * tokens, 2 * width), F32),
            jax.ShapeDtypeStruct((seq_count, tokens, width), BF16),
            jax.ShapeDtypeStruct((seq_count, ROWS, width), F32),
        ],
        scratch_shapes=[pltpu.VMEM((seq_count + 1, 2 * tokens, 2 * width), BF16)],
        compiler_params=small,
        cost_estimate=cost(seq_count * 12 * (2 * tokens) ** 2 * width, 6 << 20),
        name="transform",
    )(matrix, twist, my_taps, signals)
    mixed = []
    for start in starts:
        part = pl.pallas_call(
            functools.partial(back_kernel, start),
            in_specs=[VMEM] * 5,
            out_specs=VMEM,
            out_shape=jax.ShapeDtypeStruct((seq_count, half, width), BF16),
            compiler_params=small,
            cost_estimate=cost(200 * tokens * channels, 5 << 20),
            name="back",
        )(twist, gain, gates, turned, product)
        mixed.append(across(part))

    held = [
        pltpu.VMEM((channels, features), BF16),
        pltpu.SemaphoreType.DMA((features // TILE,)),
    ]
    gated, far = [], []
    for start, value in zip(starts, mixed):
        ready, part = pl.pallas_call(
            functools.partial(gate_kernel, start),
            in_specs=[SMEM] + [VMEM] * 3 + [HBM],
            out_specs=[VMEM] * 2,
            out_shape=[jax.ShapeDtypeStruct((half, channels), BF16), shape(half, BF16)],
            scratch_shapes=[pltpu.VMEM((2, half + ROWS, width), F32)] + held,
            compiler_params=params,
            cost_estimate=cost(2 * tokens * channels * features, 2 * channels * features),
            name="gate",
        )(me, value, branches[1], taps, out_weight)
        other = exchanged(part, 1)
        own = pl.pallas_call(
            own_kernel,
            in_specs=[SMEM, VMEM, HBM],
            out_specs=VMEM,
            out_shape=shape(half, F32),
            scratch_shapes=held,
            compiler_params=params,
            cost_estimate=cost(2 * tokens * channels * features, 2 * channels * features),
            name="own",
        )(me, ready, out_weight)
        sent = (own + other.astype(F32)).astype(BF16)
        gated.append(ready)
        far.append(exchanged(sent, 2))
    gated[0], sent = lax.optimization_barrier((gated[0], sent))
    near_part, near_own = pl.pallas_call(
        near_kernel,
        in_specs=[SMEM, VMEM, HBM],
        out_specs=[VMEM] * 2,
        out_shape=[shape(tokens, BF16), shape(tokens, F32)],
        scratch_shapes=[
            pltpu.VMEM((2, channels, features), BF16),
            pltpu.SemaphoreType.DMA((2, features // TILE)),
        ],
        compiler_params=params,
        cost_estimate=cost(4 * tokens * channels * features, 4 * channels * features),
        name="near",
    )(me, *gated, out_weight)
    near = near_own + exchanged(near_part, 1).astype(F32)
    return (near + far[0].astype(F32)).astype(BF16)


def solution(mesh):
    return jax.shard_map(
        shards,
        mesh=mesh,
        in_specs=(
            P(None, "seq", "mp"),
            P(None, "mp", None),
            P("seq", "mp"),
            P("mp"),
            P("mp", None),
        ),
        out_specs=P("seq", "mp"),
        check_vma=False,
    )
```

time: 109 us -> 98.4 us (0.903)
  starting transfers between devices: 17.2 us -> 12.8 us
  waiting for transfers between devices: 63.2 us -> 58.9 us
  local copies, waits for them, and re-layouts: 2.6 us -> 1.17 us
    ppermute x1 -> x0, starting transfers between devices: 4.84 us -> none  [shards(): lax.ppermute(branches[:, tokens - (tap_count - 1):, :], 'seq', [(s, s + 1...]
    ppermute x3, waiting for transfers between devices: 23.6 us -> 18.9 us  [exchanged(): return lax.ppermute(value, 'mp', [(m, m ^ bit) for m in range(mp_count)])]
    all_to_all x2, waiting for transfers between devices: 38.2 us -> 40 us  [across(): return lax.all_to_all(value, 'seq', 0, 0, tiled=True)]
    ppermute x1 -> x0, waiting for transfers between devices: 1.39 us -> none  [shards(): lax.ppermute(branches[:, tokens - (tap_count - 1):, :], 'seq', [(s, s + 1...]
    pallas_call x4 -> x6, Pallas kernels: 23.3 us -> 23.4 us  [the longest x1 6.13 us: shards(): pl.pallas_call(transform_kernel, in_specs=[VMEM] * 4, out_specs=[VMEM] *...]
  transfers between devices with their start and end apart: 6 -> 5, of which waited for: 5 -> 3; matrix products, arithmetic and copies ran while one was open for 1% -> 1% of each run, Pallas kernels for 7% -> 8%
where the time goes in v1:
time: 98.4 us; the launch traced here: 98.1 us
  waiting for transfers between devices  58.9 us (60%)
  Pallas kernels  23.4 us (24%)
  starting transfers between devices  12.8 us (13%)
  other arithmetic  1.81 us (2%)
  local copies, waits for them, and re-layouts  1.17 us (1%)
    all_to_all x2, waiting for transfers between devices, across(): return lax.all_to_all(value, 'seq', 0, 0, tiled=True)  40 us
    ppermute x3, waiting for transfers between devices, exchanged(): return lax.ppermute(value, 'mp', [(m, m ^ bit) for m in range(mp_count)])  18.9 us
    all_to_all x2, starting transfers between devices, across(): return lax.all_to_all(value, 'seq', 0, 0, tiled=True)  10.9 us
    pallas_call x1, Pallas kernels, shards(): pl.pallas_call(transform_kernel, in_specs=[VMEM] * 4, out_specs=[VMEM] *...  6.13 us
    pallas_call x1, Pallas kernels, shards(): pl.pallas_call(near_kernel, in_specs=[SMEM, VMEM, HBM], out_specs=[VMEM]...  4.86 us
    pallas_call x1, Pallas kernels, signals_of(): pl.pallas_call(product_kernel, in_specs=[VMEM] * 3, out_specs=VMEM, out_s...  3.38 us
    pallas_call x1, Pallas kernels, shards(): pl.pallas_call(functools.partial(gate_kernel, start), in_specs=[SMEM] + [...  3.03 us
    pallas_call x1, Pallas kernels, shards(): pl.pallas_call(own_kernel, in_specs=[SMEM, VMEM, HBM], out_specs=VMEM, ou...  3.03 us
  transfers between devices with their start and end apart: 5, of which 3 were waited for; matrix products, arithmetic and copies ran while one was open for 1% of the time, Pallas kernels for 8%

profile of v1, /device:TPU:0, one launch (start us, length us, event | category | flops | bytes accessed | tf_op | source)
XLA Modules:
  0.0 98.1 jit_solution(6779259750613376842)
XLA Ops:
  0.0 0.0 copy-start
  0.0 0.0 copy-start.1
  0.0 0.0 copy-start.2
  0.0 0.0 copy-start.3
  0.0 3.4 %product.1 = bf16[8,528,128]{2,1,0:T(8,128)(2,1)} custom-call(bf16[3,256,1024]{2,1,0:T(8,128)(2,1)} %branches.1, f32[3,3,1024]{2,1,0:T(4,128)} %bitcast.8, bf16[256,1024]{1,0:T(8,128)(2,1)} %filt.1), custom_call_target="tpu_custom_call" | custom-call | flops 10485760 | bytes 2621440 | tf_op jit(solution)/shard_map/product/pallas_call | solution.py:149
  3.4 7.3 %all-to-all-start = ((bf16[8,528,128]{2,1,0:T(8,128)(2,1)}), bf16[8,528,128]{2,1,0:T(8,128)(2,1)S(1)}, u32[]{:S(2)}, u32[]{:S(2)}) async-start(bf16[8,528,128]{2,1,0:T(8,128)(2,1)} %product.1), calls=%async_computation | async-start | bytes 2162688 | tf_op jit(solution)/shard_map/all_to_all | solution.py:359
  10.7 0.0 copy-done
  10.7 0.1 dynamic-slice_bitcast_fusion.1.gain
  10.7 0.0 copy-done.1
  10.8 26.4 %all-to-all-done.signals = bf16[8,528,128]{2,1,0:T(8,128)(2,1)S(1)} async-done(((bf16[8,528,128]{2,1,0:T(8,128)(2,1)}), bf16[8,528,128]{2,1,0:T(8,128)(2,1)S(1)}, u32[]{:S(2)}, u32[]{:S(2)}) %all-to-all-start) | async-done | bytes 1081376 | tf_op jit(solution)/shard_map/all_to_all | solution.py:359
  37.1 0.0 copy-done.2
  37.1 0.0 copy-done.3
  37.1 6.1 %transform.1 = (f32[5,512,256]{2,1,0:T(8,128)S(1)}, bf16[8,256,128]{2,1,0:T(8,128)(2,1)S(1)}, f32[8,16,128]{2,1,0:T(8,128)S(1)}) custom-call(bf16[512,512]{1,0:T(8,128)(2,1)S(1)} %copy-done.3, f32[256,32]{1,0:T(8,128)S(1)} %copy-done.2, f32[3,3,128]{2,1,0:T(4,128)S(1)} %dynamic-slice_bitcast_fusion.taps, bf16[8,528,128]{2,1,0:T(8,128)(2,1)S(1)} %all-to-all-done.signals), custom_call_target="tpu_custom_call" | custom-call | flops 3221225472 | bytes 6291456 | tf_op jit(solution)/shard_map/transform/pallas_call | solution.py:371
  43.3 2.9 %back.1 = bf16[8,256,128]{2,1,0:T(8,128)(2,1)} custom-call(f32[256,32]{1,0:T(8,128)S(1)} %copy-done.2, f32[1,128]{1,0:T(1,128)S(1)} %dynamic-slice_bitcast_fusion.1.gain, f32[8,16,128]{2,1,0:T(8,128)S(1)} %get-tuple-element.13.gates, f32[5,512,256]{2,1,0:T(8,128)S(1)} %get-tuple-element.14.turned, bf16[8,256,128]{2,1,0:T(8,128)(2,1)S(1)} %get-tuple-element.15.product), custom_call_target="tpu_custom_call" | custom-call | flops 52428800 | bytes 5242880 | tf_op jit(solution)/shard_map/back/pallas_call | solution.py:387
  46.2 3.6 %all-to-all-start.1 = ((bf16[8,256,128]{2,1,0:T(8,128)(2,1)}), bf16[8,256,128]{2,1,0:T(8,128)(2,1)S(1)}, u32[]{:S(2)}, u32[]{:S(2)}) async-start(bf16[8,256,128]{2,1,0:T(8,128)(2,1)} %back.1), calls=%async_computation.1 | async-start | bytes 1048576 | tf_op jit(solution)/shard_map/all_to_all | solution.py:359
  49.8 1.1 %slice_bitcast_fusion.branch = bf16[256,1024]{1,0:T(8,128)(2,1)S(1)} fusion(bf16[3,256,1024]{2,1,0:T(8,128)(2,1)} %branches.1), kind=kLoop, calls=%fused_computation.2 | loop fusion | bytes 1048576 | tf_op jit(solution)/shard_map/squeeze | solution.py:413
  50.9 13.6 %all-to-all-done.1.mixed = bf16[8,256,128]{2,1,0:T(8,128)(2,1)S(1)} async-done(((bf16[8,256,128]{2,1,0:T(8,128)(2,1)}), bf16[8,256,128]{2,1,0:T(8,128)(2,1)S(1)}, u32[]{:S(2)}, u32[]{:S(2)}) %all-to-all-start.1) | async-done | bytes 524320 | tf_op jit(solution)/shard_map/all_to_all | solution.py:359
  64.5 3.0 %gate.1 = (bf16[256,1024]{1,0:T(8,128)(2,1)S(1)}, bf16[256,2048]{1,0:T(8,128)(2,1)S(1)}) custom-call(s32[1]{0:T(128)} %bitcast.place, bf16[8,256,128]{2,1,0:T(8,128)(2,1)S(1)} %all-to-all-done.1.mixed, bf16[256,1024]{1,0:T(8,128)(2,1)S(1)} %slice_bitcast_fusion.branch, f32[3,3,1024]{2,1,0:T(4,128)S(1)} %bitcast.9, bf16[1024,8192]{1,0:T(8,128)(2,1)} %weight.5), custom_call_target="tpu_custom_call" | custom-call | flops 1073741824 | bytes 4194304 | tf_op jit(solution)/shard_map/gate/pallas_call | solution.py:404
  67.5 0.1 collective-permute-start
  67.6 3.0 %own.1 = f32[256,2048]{1,0:T(8,128)S(1)} custom-call(s32[1]{0:T(128)} %bitcast.place, bf16[256,1024]{1,0:T(8,128)(2,1)S(1)} %get-tuple-element.18.gated, bf16[1024,8192]{1,0:T(8,128)(2,1)} %weight.5), custom_call_target="tpu_custom_call" | custom-call | flops 1073741824 | bytes 4194304 | tf_op jit(solution)/shard_map/own/pallas_call | solution.py:415
  70.6 0.0 collective-permute-done
  70.6 0.3 add_convert_fusion.1
  71.0 1.6 %collective-permute-start.2 = (bf16[256,2048]{1,0:T(8,128)(2,1)S(1)}, bf16[256,2048]{1,0:T(8,128)(2,1)S(1)}, u32[]{:S(2)}, u32[]{:S(2)}) collective-permute-start(bf16[256,2048]{1,0:T(8,128)(2,1)S(1)} %add_convert_fusion.1), channel_id=1, source_target_pairs={{0,2},{1,3},{2,0},{3,1},{4,6},{5,7},{6,4},{7,5},{8,10},{9,11},{10,... | collective-permute-start | bytes 3145736 | tf_op jit(solution)/shard_map/ppermute | solution.py:356
  72.5 4.9 %near.1 = (bf16[256,2048]{1,0:T(8,128)(2,1)S(1)}, f32[256,2048]{1,0:T(8,128)S(1)}) custom-call(s32[1]{0:T(128)} %bitcast.place, bf16[256,1024]{1,0:T(8,128)(2,1)S(1)} %get-tuple-element.18.gated, bf16[1024,8192]{1,0:T(8,128)(2,1)} %weight.5), custom_call_target="tpu_custom_call" | custom-call | flops 2147483648 | bytes 8388608 | tf_op jit(solution)/shard_map/near/pallas_call | solution.py:429
  77.4 0.3 collective-permute-start.1
  77.7 18.9 %collective-permute-done.2 = bf16[256,2048]{1,0:T(8,128)(2,1)S(1)} collective-permute-done((bf16[256,2048]{1,0:T(8,128)(2,1)S(1)}, bf16[256,2048]{1,0:T(8,128)(2,1)S(1)}, u32[]{:S(2)}, u32[]{:S(2)}) %collective-permute-start.2) | collective-permute-done | bytes 1048608 | tf_op jit(solution)/shard_map/ppermute | solution.py:356
  96.6 0.0 collective-permute-done.1
  96.6 1.5 %add_convert_fusion = bf16[256,2048]{1,0:T(8,128)(2,1)} fusion(bf16[256,2048]{1,0:T(8,128)(2,1)S(1)} %collective-permute-done.2, f32[256,2048]{1,0:T(8,128)S(1)} %get-tuple-element.19, bf16[256,2048]{1,0:T(8,128)(2,1)S(1)} %collective-permute-done.1), kind=kLoop, calls=%fused_computation | loop fusion | flops 2621440 | bytes 5242880 | tf_op jit(solution)/shard_map/convert_element_type | solution.py:443
  (1 shorter events, 0.0 us)
Async XLA Ops:
  0.0 10.7 %copy-start = (f32[1024]{0:T(1024)S(1)}, f32[1024]{0:T(1024)}, u32[]{:S(2)}) copy-start(f32[1024]{0:T(1024)} %param.10) | copy-start | bytes 12292
  0.0 10.7 %copy-start.1 = (f32[3,1024,3]{1,2,0:T(4,128)S(1)}, f32[3,1024,3]{1,2,0:T(4,128)}, u32[]{:S(2)}) copy-start(f32[3,1024,3]{1,2,0:T(4,128)} %param.8) | copy-start | bytes 110596
  0.0 37.1 %copy-start.2 = (f32[256,32]{1,0:T(8,128)S(1)}, f32[256,32]{1,0:T(8,128)}, u32[]{:S(2)}) copy-start(f32[256,32]{1,0:T(8,128)} %constant.20.clone.twist) | copy-start | bytes 98308
  0.0 37.1 %copy-start.3 = (bf16[512,512]{1,0:T(8,128)(2,1)S(1)}, bf16[512,512]{1,0:T(8,128)(2,1)}, u32[]{:S(2)}) copy-start(bf16[512,512]{1,0:T(8,128)(2,1)} %constant.19.clone.matrix) | copy-start | bytes 1572868
  3.4 33.7 %all-to-all-start = ((bf16[8,528,128]{2,1,0:T(8,128)(2,1)}), bf16[8,528,128]{2,1,0:T(8,128)(2,1)S(1)}, u32[]{:S(2)}, u32[]{:S(2)}) async-start(bf16[8,528,128]{2,1,0:T(8,128)(2,1)} %product.1), calls=%async_computation | async-start | bytes 2162688 | tf_op jit(solution)/shard_map/all_to_all | solution.py:359
  46.2 18.3 %all-to-all-start.1 = ((bf16[8,256,128]{2,1,0:T(8,128)(2,1)}), bf16[8,256,128]{2,1,0:T(8,128)(2,1)S(1)}, u32[]{:S(2)}, u32[]{:S(2)}) async-start(bf16[8,256,128]{2,1,0:T(8,128)(2,1)} %back.1), calls=%async_computation.1 | async-start | bytes 1048576 | tf_op jit(solution)/shard_map/all_to_all | solution.py:359
  67.5 3.1 %collective-permute-start = (bf16[256,2048]{1,0:T(8,128)(2,1)S(1)}, bf16[256,2048]{1,0:T(8,128)(2,1)S(1)}, u32[]{:S(2)}, u32[]{:S(2)}) collective-permute-start(bf16[256,2048]{1,0:T(8,128)(2,1)S(1)} %get-tuple-element.17), channel_id=1, source_target_pairs={{0,1},{1,0},{2,3},{3,2},{4,5},{5,4},{6,7},{7,6},{8,9},{9,8},{10,11... | collective-permute-start | bytes 3145736 | tf_op jit(solution)/shard_map/ppermute | solution.py:356
  71.0 25.6 %collective-permute-start.2 = (bf16[256,2048]{1,0:T(8,128)(2,1)S(1)}, bf16[256,2048]{1,0:T(8,128)(2,1)S(1)}, u32[]{:S(2)}, u32[]{:S(2)}) collective-permute-start(bf16[256,2048]{1,0:T(8,128)(2,1)S(1)} %add_convert_fusion.1), channel_id=1, source_target_pairs={{0,2},{1,3},{2,0},{3,1},{4,6},{5,7},{6,4},{7,5},{8,10},{9,11},{10,... | collective-permute-start | bytes 3145736 | tf_op jit(solution)/shard_map/ppermute | solution.py:356
  77.4 19.2 %collective-permute-start.1 = (bf16[256,2048]{1,0:T(8,128)(2,1)S(1)}, bf16[256,2048]{1,0:T(8,128)(2,1)S(1)}, u32[]{:S(2)}, u32[]{:S(2)}) collective-permute-start(bf16[256,2048]{1,0:T(8,128)(2,1)S(1)} %get-tuple-element.20), channel_id=1, source_target_pairs={{0,1},{1,0},{2,3},{3,2},{4,5},{5,4},{6,7},{7,6},{8,9},{9,8},{10,11... | collective-permute-start | bytes 3145736 | tf_op jit(solution)/shard_map/ppermute | solution.py:356

commit v2 on v1

--- a/solution.py
+++ b/solution.py
@@ -42,21 +42,31 @@
     return math.cos(angle), math.sin(angle)
 
 
+def combined(signs, terms):
+    total = None
+    for sign, term in zip(signs, terms):
+        if term is not None:
+            total = axpy(total, sign, term)
+    return total
+
+
 def across_blocks(values):
     count = len(values)
     radix, half = 2 * count, count // 2
     sums = {n: values[n] + values[count - n] for n in range(1, half)}
     diffs = {n: values[n] - values[count - n] for n in range(1, half)}
-    result = []
-    for k in range(count + 1):
+    result = [None] * (count + 1)
+    for k in range(half + 1):
         in_cos, in_sin = (sums, diffs) if k % 2 == 0 else (diffs, sums)
-        real = axpy(values[0], wave(half * k, radix)[0], values[half])
-        imag = axpy(None, -wave(half * k, radix)[1], values[half])
+        real = [axpy(values[0], wave(half * k, radix)[0], values[half]), None]
+        imag = [axpy(None, -wave(half * k, radix)[1], values[half]), None]
         for n in range(1, half):
             cosine, sine = wave(n * k, radix)
-            real = axpy(real, cosine, in_cos[n])
-            imag = axpy(imag, -sine, in_sin[n])
-        result.append((real, imag))
+            real[n % 2] = axpy(real[n % 2], cosine, in_cos[n])
+            imag[n % 2] = axpy(imag[n % 2], -sine, in_sin[n])
+        result[k] = (combined([1, 1], real), combined([1, 1], imag))
+        if k < half:
+            result[count - k] = (combined([1, -1], real), combined([-1, 1], imag))
     return result
 
 
@@ -77,26 +87,19 @@
                 odd_cos = axpy(odd_cos, cosine, real)
                 odd_sin = axpy(odd_sin, -sine, imag)
 
-        def combined(terms):
-            total = None
-            for sign, term in terms:
-                if term is not None:
-                    total = axpy(total, sign, term)
-            return total
-
-        result[n] = combined([(1, even_cos), (1, even_sin), (1, odd_cos), (1, odd_sin)])
+        terms = (even_cos, even_sin, odd_cos, odd_sin)
+        result[n] = combined((1, 1, 1, 1), terms)
         if 0 < n < half:
-            result[count - n] = combined(
-                [(1, even_cos), (-1, even_sin), (-1, odd_cos), (1, odd_sin)]
-            )
+            result[count - n] = combined((1, -1, -1, 1), terms)
     return result
 
 
 VMEM = pl.BlockSpec(memory_space=pltpu.VMEM)
 SMEM = pl.BlockSpec(memory_space=pltpu.SMEM)
 HBM = pl.BlockSpec(memory_space=pltpu.HBM)
-STRIP = 64
 TILE = 512
+PIECES = 8
+STEPS = 4
 BRANCHES = 3
 
 
@@ -104,57 +107,98 @@
     return pl.CostEstimate(flops=int(flops), bytes_accessed=int(moved), transcendentals=0)
 
 
-def smoothed(block, taps, lanes, padded, start, rows):
+def smoothed(block, lanes, taps, padded, rows, start=0):
     if start == 0:
         padded[:ROWS, :] = jnp.zeros((ROWS, padded.shape[1]), F32)
     else:
         padded[:ROWS, :] = block[start - ROWS : start, lanes].astype(F32)
-    strip = min(STRIP, rows)
+    strip = next(n for n in (64, 32, 16) if rows % n == 0)
     for begin in range(0, rows, strip):
         value = block[start + begin : start + begin + strip, lanes].astype(F32)
         padded[ROWS + begin : ROWS + begin + strip, :] = value
     for begin in range(0, rows, strip):
         total = None
-        for tap in range(taps.shape[0]):
+        for tap in range(len(taps)):
             first = ROWS - tap + begin
-            term = padded[first : first + strip, :] * taps[tap : tap + 1, lanes]
+            term = padded[first : first + strip, :] * taps[tap]
             total = term if total is None else total + term
         yield slice(begin, begin + strip), total
 
 
-def product_kernel(branches, taps, filt, out, padded):
-    parts, width = out.shape[0], out.shape[2]
+def tap_rows(taps, branch, lanes):
+    return [taps[branch, tap : tap + 1, lanes] for tap in range(taps.shape[1])]
+
+
+def product_kernel(all_taps, branches, filt, out, taps, held, rims, ready, padded, ins, ends, outs):
+    parts, height, width = out.shape
     rows, edge = filt.shape[0], taps.shape[1] - 1
+    copies = [pltpu.make_async_copy(all_taps, taps, ends.at[2])]
+    for side in (0, 1):
+        source = branches.at[1, pl.ds(side * (rows - ROWS), ROWS), :]
+        copies.append(pltpu.make_async_copy(source, rims.at[side], ends.at[side]))
+    for i, source in enumerate((branches.at[0], branches.at[2], filt)):
+        copies.append(pltpu.make_async_copy(source, held.at[i], ins.at[i]))
+    for copy in copies:
+        copy.start()
+    for copy in copies:
+        copy.wait()
+    first, third, kept = (held.at[i] for i in range(3))
+    sent = []
     for j in range(parts):
         lanes = slice(j * width, (j + 1) * width)
-        first, third = (
-            smoothed(branches.at[b], taps.at[b], lanes, padded.at[j % 2, b // 2], 0, rows)
-            for b in (0, 2)
+        pair = (
+            smoothed(block, lanes, tap_rows(taps, b, lanes), padded.at[j % 2, b // 2], rows)
+            for block, b in ((first, 0), (third, 2))
         )
-        for (span, left), (span, right) in zip(first, third):
-            out[j, span, :] = (left * right).astype(BF16)
-        out[j, rows : 2 * rows, :] = filt[:, lanes]
-        rims = [branches[b, rows - ROWS :, lanes].astype(F32)[-edge:] for b in range(BRANCHES)]
-        rims += [branches[b, :ROWS, lanes].astype(F32)[:edge] for b in range(BRANCHES)]
-        unused = out.shape[1] - 2 * rows - 2 * BRANCHES * edge
+        for (span, left), (span, right) in zip(*pair):
+            ready[j, span, :] = (left * right).astype(BF16)
+        ready[j, rows : 2 * rows, :] = kept[:, lanes]
+        tails = [
+            first[rows - ROWS :, lanes].astype(F32)[-edge:],
+            rims[1, :, lanes].astype(F32)[-edge:],
+            third[rows - ROWS :, lanes].astype(F32)[-edge:],
+            first[:ROWS, lanes].astype(F32)[:edge],
+            rims[0, :, lanes].astype(F32)[:edge],
+            third[:ROWS, lanes].astype(F32)[:edge],
+        ]
+        unused = height - 2 * rows - 2 * BRANCHES * edge
         if unused:
-            rims.append(jnp.zeros((unused, width), F32))
-        out[j, 2 * rows :, :] = jnp.concatenate(rims, axis=0).astype(BF16)
+            tails.append(jnp.zeros((unused, width), F32))
+        ready[j, 2 * rows :, :] = jnp.concatenate(tails, axis=0).astype(BF16)
+        copy = pltpu.make_async_copy(ready.at[j], out.at[j], outs.at[j])
+        copy.start()
+        sent.append(copy)
+    for copy in sent:
+        copy.wait()
 
 
 def signals_of(branches, taps, filt, parts):
     rows, channels = filt.shape
     width = channels // parts
-    rims = -(-2 * BRANCHES * (taps.shape[1] - 1) // ROWS) * ROWS
+    height = 2 * rows - (-2 * BRANCHES * (taps.shape[1] - 1) // ROWS) * ROWS
     return pl.pallas_call(
         product_kernel,
-        in_specs=[VMEM] * 3,
-        out_specs=VMEM,
-        out_shape=jax.ShapeDtypeStruct((parts, 2 * rows + rims, width), BF16),
-        scratch_shapes=[pltpu.VMEM((2, 2, rows + ROWS, width), F32)],
+        in_specs=[HBM] * 3,
+        out_specs=HBM,
+        out_shape=jax.ShapeDtypeStruct((parts, height, width), BF16),
+        scratch_shapes=[
+            pltpu.VMEM(taps.shape, F32),
+            pltpu.VMEM((3, rows, channels), BF16),
+            pltpu.VMEM((2, ROWS, channels), BF16),
+            pltpu.VMEM((parts, height, width), BF16),
+            pltpu.VMEM((2, 2, rows + ROWS, width), F32),
+            pltpu.SemaphoreType.DMA((3,)),
+            pltpu.SemaphoreType.DMA((3,)),
+            pltpu.SemaphoreType.DMA((parts,)),
+        ],
+        compiler_params=pltpu.CompilerParams(vmem_limit_bytes=62 << 20),
         cost_estimate=cost(40 * rows * channels, 10 * rows * channels),
         name="product",
-    )(branches, taps, filt)
+    )(taps, branches, filt)
+
+
+def unrolled(blocks):
+    return 4 if blocks <= 8 else 1
 
 
 def chunk_of(index, offset=0):
@@ -208,6 +252,10 @@
 
     def forward(index, carry):
         rows, low = chunk_of(index), chunk_of(index, length)
+        turns = [
+            (column(twist, rows, k, width), column(twist, rows, blocks + k, width))
+            for k in range(blocks)
+        ]
         for side in (0, 1):
             lanes = slice(side * width, (side + 1) * width)
             if side == 0:
@@ -218,8 +266,7 @@
             waves[0, rows, lanes] = spectra[0][0].astype(BF16)
             for k in range(1, blocks + 1):
                 real, imag = spectra[k]
-                cosine = column(twist, rows, k - 1, width)
-                sine = column(twist, rows, blocks + k - 1, width)
+                cosine, sine = turns[k - 1]
                 if imag is None:
                     waves[k, rows, lanes] = (real * cosine).astype(BF16)
                     waves[k, low, lanes] = (-real * sine).astype(BF16)
@@ -228,7 +275,7 @@
                     waves[k, low, lanes] = (imag * cosine - real * sine).astype(BF16)
         return carry
 
-    lax.fori_loop(0, length // ROWS, forward, 0)
+    lax.fori_loop(0, length // ROWS, forward, 0, unroll=unrolled(blocks))
 
     def multiplied(spectrum):
         real, imag = spectrum[:length], spectrum[length:]
@@ -260,13 +307,12 @@
         lax.fori_loop(0, pairs, lambda pair, carry: (one_pair(pair), carry)[1], 0)
 
 
-def back_kernel(start, twist, gain, gates, turned, product, out):
-    blocks, count, width = out.shape
-    length = product.shape[1]
+def back_kernel(twist, gain, gates, turned, product, *outs):
+    blocks, length, width = product.shape
     full, pairs = 2 * blocks * length, blocks // 2
     skip = jnp.broadcast_to(gain[...], (ROWS, width))
 
-    def backward(index, carry):
+    def backward(out, start, index, carry):
         rows, low = chunk_of(index, start), chunk_of(index, length + start)
         parts = []
         for k in range(1, blocks + 1):
@@ -283,38 +329,56 @@
             out[b, chunk_of(index), :] = (value + direct).astype(BF16)
         return carry
 
-    lax.fori_loop(0, count // ROWS, backward, 0)
-    if start == 0:
-        for b in range(blocks):
-            out[b, :ROWS, :] = (out[b, :ROWS, :].astype(F32) * gates[b]).astype(BF16)
+    start = 0
+    for out in outs:
+        body = functools.partial(backward, out, start)
+        lax.fori_loop(0, out.shape[1] // ROWS, body, 0, unroll=unrolled(blocks))
+        start += out.shape[1]
+    for b in range(blocks):
+        outs[0][b, :ROWS, :] = (outs[0][b, :ROWS, :].astype(F32) * gates[b]).astype(BF16)
 
 
 def weight_copies(weight, held, sems, block):
-    columns = held.shape[1]
-    result = []
-    for index, start in enumerate(range(0, columns, TILE)):
-        span = pl.ds(pl.multiple_of(block * columns + start, TILE), TILE)
-        target = held.at[:, start : start + TILE]
-        result.append(pltpu.make_async_copy(weight.at[:, span], target, sems.at[index]))
-    return result
-
-
-def project_into(out, gated, held, copies):
-    for copy, start in zip(copies, range(0, out.shape[1], TILE)):
-        span = slice(start, start + TILE)
-        copy.wait()
-        value = jnp.dot(gated, held[:, span], preferred_element_type=F32)
-        out[:, span] = value.astype(out.dtype)
-
-
-def gate_kernel(start, place, mixed, branch, taps, weight, gated, part, padded, held, sems):
-    copies = weight_copies(weight, held, sems, place[0] ^ 3)
+    depth, columns = held.shape
+    span = pl.ds(pl.multiple_of(block * columns, columns), columns)
+    step = depth // PIECES
+    pieces = [pl.ds(i * step, step) for i in range(PIECES)]
+    return [
+        pltpu.make_async_copy(weight.at[rows, span], held.at[rows, :], sems.at[i])
+        for i, rows in enumerate(pieces)
+    ]
+
+
+def start_all(copies):
     for copy in copies:
         copy.start()
+
+
+def project_into(outs, gated, weight, copies, total):
+    depth, columns = weight.shape
+    group = PIECES // STEPS
+    for step in range(STEPS):
+        for copy in copies[step * group : (step + 1) * group]:
+            copy.wait()
+        rows = slice(step * depth // STEPS, (step + 1) * depth // STEPS)
+        for start in range(0, columns, TILE):
+            span = slice(start, start + TILE)
+            value = jnp.dot(gated[:, rows], weight[rows, span], preferred_element_type=F32)
+            if step:
+                value = total[:, span] + value
+            if step < STEPS - 1:
+                total[:, span] = value
+            else:
+                index, offset = divmod(start, columns // len(outs))
+                out = outs[index]
+                out[:, offset : offset + TILE] = value.astype(out.dtype)
+
+
+def gated_rows(start, mixed, branch, taps, gated, padded):
     parts, rows, width = mixed.shape
     for j in range(parts):
         lanes = slice(j * width, (j + 1) * width)
-        strips = smoothed(branch, taps.at[1], lanes, padded.at[j % 2], start, rows)
+        strips = smoothed(branch, lanes, tap_rows(taps, 1, lanes), padded.at[j % 2], rows, start)
         for span, second in strips:
             value = mixed[j, span, :].astype(F32)
             done = second * value
@@ -322,23 +386,31 @@
                 ids = lax.broadcasted_iota(jnp.int32, done.shape, 0)
                 done = jnp.where(ids < taps.shape[1] - 1, value, done)
             gated[span, lanes] = done.astype(BF16)
-    project_into(part, gated[...], held, copies)
-
-
-def own_kernel(place, gated, weight, own, held, sems):
-    copies = weight_copies(weight, held, sems, place[0] ^ 2)
-    for copy in copies:
-        copy.start()
-    project_into(own, gated[...], held, copies)
-
-
-def near_kernel(place, gated, weight, part, own, held, sems):
+
+
+def gate_kernel(start, place, mixed, branch, taps, weight, gated, part, padded, held, sems, total):
+    copies = weight_copies(weight, held.at[0], sems.at[0], place[0] ^ 3)
+    start_all(copies)
+    gated_rows(start, mixed, branch, taps, gated, padded)
+    project_into([part], gated, held.at[0], copies, total)
+
+
+def own_kernel(place, gated, weight, own, held, sems, total):
+    copies = weight_copies(weight, held.at[0], sems.at[0], place[0] ^ 2)
+    start_all(copies)
+    project_into([own], gated, held.at[0], copies, total)
+
+
+def near_kernel(place, first, second, weight, *rest):
+    *parts, own, held, sems, total, gated = rest
     sets = [weight_copies(weight, held.at[i], sems.at[i], place[0] ^ (1 - i)) for i in (0, 1)]
-    for copies in sets:
-        for copy in copies:
-            copy.start()
-    for i, out in enumerate((part, own)):
-        project_into(out, gated[...], held.at[i], sets[i])
+    start_all(sets[0])
+    start_all(sets[1])
+    rows = first.shape[0]
+    gated[:rows, :] = first[...]
+    gated[rows:, :] = second[...]
+    project_into(parts, gated, held.at[0], sets[0], total)
+    project_into([own], gated, held.at[1], sets[1], total)
 
 
 def shards(branches, short_filter, long_filter, skip_gain, out_weight):
@@ -349,8 +421,6 @@
     me, place = lax.axis_index("mp").reshape(1), lax.axis_index("seq")
     params = pltpu.CompilerParams(vmem_limit_bytes=50 << 20)
     small = pltpu.CompilerParams(vmem_limit_bytes=24 << 20)
-    half = tokens
-    starts = (0,)
 
     def exchanged(value, bit):
         return lax.ppermute(value, "mp", [(m, m ^ bit) for m in range(mp_count)])
@@ -358,7 +428,7 @@
     def across(value):
         return lax.all_to_all(value, "seq", 0, 0, tiled=True)
 
-    def shape(rows, dtype):
+    def shape(dtype, rows):
         return jax.ShapeDtypeStruct((rows, features), dtype)
 
     taps = jnp.transpose(short_filter, (0, 2, 1))
@@ -382,33 +452,36 @@
         cost_estimate=cost(seq_count * 12 * (2 * tokens) ** 2 * width, 6 << 20),
         name="transform",
     )(matrix, twist, my_taps, signals)
-    mixed = []
-    for start in starts:
-        part = pl.pallas_call(
-            functools.partial(back_kernel, start),
-            in_specs=[VMEM] * 5,
-            out_specs=VMEM,
-            out_shape=jax.ShapeDtypeStruct((seq_count, half, width), BF16),
-            compiler_params=small,
-            cost_estimate=cost(200 * tokens * channels, 5 << 20),
-            name="back",
-        )(twist, gain, gates, turned, product)
-        mixed.append(across(part))
-
-    held = [
-        pltpu.VMEM((channels, features), BF16),
-        pltpu.SemaphoreType.DMA((features // TILE,)),
-    ]
+    counts = (tokens * 128 // 256, tokens * 128 // 256)
+    mixed = pl.pallas_call(
+        back_kernel,
+        in_specs=[VMEM] * 5,
+        out_specs=[VMEM] * len(counts),
+        out_shape=[jax.ShapeDtypeStruct((seq_count, count, width), BF16) for count in counts],
+        compiler_params=small,
+        cost_estimate=cost(200 * tokens * channels, 5 << 20),
+        name="back",
+    )(twist, gain, gates, turned, product)
+    mixed = [across(part) for part in mixed]
+
+    flops, moved = 2 * tokens * channels * features, 2 * channels * features
+    held = pltpu.VMEM((2, channels, features), BF16)
+    sems = pltpu.SemaphoreType.DMA((2, PIECES))
     gated, far = [], []
-    for start, value in zip(starts, mixed):
+    start = 0
+    for step, (value, count) in enumerate(zip(mixed, counts)):
+        padded = pltpu.VMEM((2, count + ROWS, width), F32)
+        total = pltpu.VMEM((count, features), F32)
+        if step:
+            value, sent = lax.optimization_barrier((value, sent))
         ready, part = pl.pallas_call(
             functools.partial(gate_kernel, start),
             in_specs=[SMEM] + [VMEM] * 3 + [HBM],
             out_specs=[VMEM] * 2,
-            out_shape=[jax.ShapeDtypeStruct((half, channels), BF16), shape(half, BF16)],
-            scratch_shapes=[pltpu.VMEM((2, half + ROWS, width), F32)] + held,
+            out_shape=[jax.ShapeDtypeStruct((count, channels), BF16), shape(BF16, count)],
+            scratch_shapes=[padded, held, sems, total],
             compiler_params=params,
-            cost_estimate=cost(2 * tokens * channels * features, 2 * channels * features),
+            cost_estimate=cost(1, 1),
             name="gate",
         )(me, value, branches[1], taps, out_weight)
         other = exchanged(part, 1)
@@ -416,31 +489,39 @@
             own_kernel,
             in_specs=[SMEM, VMEM, HBM],
             out_specs=VMEM,
-            out_shape=shape(half, F32),
-            scratch_shapes=held,
+            out_shape=shape(F32, count),
+            scratch_shapes=[held, sems, total],
             compiler_params=params,
-            cost_estimate=cost(2 * tokens * channels * features, 2 * channels * features),
+            cost_estimate=cost(1, 1),
             name="own",
         )(me, ready, out_weight)
+        if step:
+            own, far[0] = lax.optimization_barrier((own, far[0]))
         sent = (own + other.astype(F32)).astype(BF16)
         gated.append(ready)
         far.append(exchanged(sent, 2))
-    gated[0], sent = lax.optimization_barrier((gated[0], sent))
-    near_part, near_own = pl.pallas_call(
+        start += count
+    gated[0], gated[1], sent = lax.optimization_barrier((gated[0], gated[1], sent))
+    pieces = 4
+    *near_part, near_own = pl.pallas_call(
         near_kernel,
-        in_specs=[SMEM, VMEM, HBM],
-        out_specs=[VMEM] * 2,
-        out_shape=[shape(tokens, BF16), shape(tokens, F32)],
+        in_specs=[SMEM, VMEM, VMEM, HBM],
+        out_specs=[VMEM] * (pieces + 1),
+        out_shape=[jax.ShapeDtypeStruct((tokens, features // pieces), BF16)] * pieces
+        + [shape(F32, tokens)],
         scratch_shapes=[
-            pltpu.VMEM((2, channels, features), BF16),
-            pltpu.SemaphoreType.DMA((2, features // TILE)),
+            held,
+            sems,
+            pltpu.VMEM((tokens, features), F32),
+            pltpu.VMEM((tokens, channels), BF16),
         ],
         compiler_params=params,
-        cost_estimate=cost(4 * tokens * channels * features, 4 * channels * features),
+        cost_estimate=cost(1, 1),
         name="near",
     )(me, *gated, out_weight)
-    near = near_own + exchanged(near_part, 1).astype(F32)
-    return (near + far[0].astype(F32)).astype(BF16)
+    near_part = jnp.concatenate([exchanged(part, 1) for part in near_part], axis=1)
+    near = near_own + near_part.astype(F32)
+    return (near + jnp.concatenate(far, axis=0).astype(F32)).astype(BF16)
 
 
 def solution(mesh):

time: 98.4 us -> 94.9 us (0.964)
  waiting for transfers between devices: 58.9 us -> 48.2 us
  starting transfers between devices: 12.8 us -> 18.9 us
  Pallas kernels: 23.4 us -> 24.4 us
    ppermute x3 -> x8, waiting for transfers between devices: 18.9 us -> 8.54 us  [exchanged(): return lax.ppermute(value, 'mp', [(m, m ^ bit) for m in range(mp_count)])]
    all_to_all x2 -> x3, starting transfers between devices: 10.9 us -> 14.5 us  [across(): return lax.all_to_all(value, 'seq', 0, 0, tiled=True)]
    ppermute x3 -> x8, starting transfers between devices: 1.94 us -> 4.4 us  [exchanged(): return lax.ppermute(value, 'mp', [(m, m ^ bit) for m in range(mp_count)])]
    pallas_call x1 -> x2, Pallas kernels: 3.03 us -> 5.23 us  [shards(): pl.pallas_call(functools.partial(gate_kernel, start), in_specs=[SMEM] + [...]
    pallas_call x1 -> x2, Pallas kernels: 3.03 us -> 5.22 us  [shards(): pl.pallas_call(own_kernel, in_specs=[SMEM, VMEM, HBM], out_specs=VMEM, ou...]
    pallas_call x3, Pallas kernels: 11.2 us -> 9.34 us  [the longest x1 4.19 us: shards(): pl.pallas_call(near_kernel, in_specs=[SMEM, VMEM, VMEM, HBM], out_specs=[...]
    pallas_call x1, Pallas kernels: 6.13 us -> 4.63 us  [shards(): pl.pallas_call(transform_kernel, in_specs=[VMEM] * 4, out_specs=[VMEM] *...]
    all_to_all x2 -> x3, waiting for transfers between devices: 40 us -> 39.7 us  [across(): return lax.all_to_all(value, 'seq', 0, 0, tiled=True)]
  transfers between devices with their start and end apart: 5 -> 11, of which waited for: 3 -> 9; matrix products, arithmetic and copies ran while one was open for 1% -> 1% of each run, Pallas kernels for 8% -> 13%
where the time goes in v2:
time: 94.9 us; the launch traced here: 94.4 us
  waiting for transfers between devices  48.2 us (51%)
  Pallas kernels  24.4 us (26%)
  starting transfers between devices  18.9 us (20%)
  other arithmetic  1.6 us (2%)
  local copies, waits for them, and re-layouts  1.17 us (1%)
    all_to_all x3, waiting for transfers between devices, across(): return lax.all_to_all(value, 'seq', 0, 0, tiled=True)  39.7 us
    all_to_all x3, starting transfers between devices, across(): return lax.all_to_all(value, 'seq', 0, 0, tiled=True)  14.5 us
    ppermute x8, waiting for transfers between devices, exchanged(): return lax.ppermute(value, 'mp', [(m, m ^ bit) for m in range(mp_count)])  8.54 us
    pallas_call x2, Pallas kernels, shards(): pl.pallas_call(functools.partial(gate_kernel, start), in_specs=[SMEM] + [...  5.23 us
    pallas_call x2, Pallas kernels, shards(): pl.pallas_call(own_kernel, in_specs=[SMEM, VMEM, HBM], out_specs=VMEM, ou...  5.22 us
    pallas_call x1, Pallas kernels, shards(): pl.pallas_call(transform_kernel, in_specs=[VMEM] * 4, out_specs=[VMEM] *...  4.63 us
    ppermute x8, starting transfers between devices, exchanged(): return lax.ppermute(value, 'mp', [(m, m ^ bit) for m in range(mp_count)])  4.4 us
    pallas_call x1, Pallas kernels, shards(): pl.pallas_call(near_kernel, in_specs=[SMEM, VMEM, VMEM, HBM], out_specs=[...  4.19 us
  transfers between devices with their start and end apart: 11, of which 9 were waited for; matrix products, arithmetic and copies ran while one was open for 1% of the time, Pallas kernels for 13%

profile of v2, /device:TPU:0, one launch (start us, length us, event | category | flops | bytes accessed | tf_op | source)
XLA Modules:
  0.0 94.4 jit_solution(1779444690110176260)
XLA Ops:
  0.0 0.0 copy-start
  0.0 0.0 copy-start.1
  0.0 0.0 copy-start.2
  0.0 0.0 copy-start.3
  0.0 3.1 %product.1 = bf16[8,528,128]{2,1,0:T(8,128)(2,1)} custom-call(f32[3,3,1024]{2,1,0:T(4,128)} %bitcast.8, bf16[3,256,1024]{2,1,0:T(8,128)(2,1)} %branches.1, bf16[256,1024]{1,0:T(8,128)(2,1)} %filt.1), custom_call_target="tpu_custom_call" | custom-call | flops 10485760 | bytes 2621440 | tf_op jit(solution)/shard_map/product/pallas_call | solution.py:179
  3.1 7.3 %all-to-all-start = ((bf16[8,528,128]{2,1,0:T(8,128)(2,1)}), bf16[8,528,128]{2,1,0:T(8,128)(2,1)S(1)}, u32[]{:S(2)}, u32[]{:S(2)}) async-start(bf16[8,528,128]{2,1,0:T(8,128)(2,1)} %product.1), calls=%async_computation | async-start | bytes 2162688 | tf_op jit(solution)/shard_map/all_to_all | solution.py:429
  10.4 0.0 copy-done
  10.4 0.1 dynamic-slice_bitcast_fusion.1.gain
  10.5 0.0 copy-done.1
  10.5 26.4 %all-to-all-done.signals = bf16[8,528,128]{2,1,0:T(8,128)(2,1)S(1)} async-done(((bf16[8,528,128]{2,1,0:T(8,128)(2,1)}), bf16[8,528,128]{2,1,0:T(8,128)(2,1)S(1)}, u32[]{:S(2)}, u32[]{:S(2)}) %all-to-all-start) | async-done | bytes 1081376 | tf_op jit(solution)/shard_map/all_to_all | solution.py:429
  36.9 0.0 copy-done.2
  36.9 0.0 copy-done.3
  36.9 4.6 %transform.1 = (f32[5,512,256]{2,1,0:T(8,128)S(1)}, bf16[8,256,128]{2,1,0:T(8,128)(2,1)S(1)}, f32[8,16,128]{2,1,0:T(8,128)S(1)}) custom-call(bf16[512,512]{1,0:T(8,128)(2,1)S(1)} %copy-done.3, f32[256,32]{1,0:T(8,128)S(1)} %copy-done.2, f32[3,3,128]{2,1,0:T(4,128)S(1)} %dynamic-slice_bitcast_fusion.taps, bf16[8,528,128]{2,1,0:T(8,128)(2,1)S(1)} %all-to-all-done.signals), custom_call_target="tpu_custom_call" | custom-call | flops 3221225472 | bytes 6291456 | tf_op jit(solution)/shard_map/transform/pallas_call | solution.py:441
  41.5 2.0 %back.1 = (bf16[8,128,128]{2,1,0:T(8,128)(2,1)}, bf16[8,128,128]{2,1,0:T(8,128)(2,1)}) custom-call(f32[256,32]{1,0:T(8,128)S(1)} %copy-done.2, f32[1,128]{1,0:T(1,128)S(1)} %dynamic-slice_bitcast_fusion.1.gain, f32[8,16,128]{2,1,0:T(8,128)S(1)} %get-tuple-element.24.gates, f32[5,512,256]{2,1,0:T(8,128)S(1)} %get-tuple-element.25.turned, ...), custom_call_target="tpu_custom_call" | custom-call | flops 52428800 | bytes 5242880 | tf_op jit(solution)/shard_map/back/pallas_call | solution.py:456
  43.6 3.6 %all-to-all-start.1 = ((bf16[8,128,128]{2,1,0:T(8,128)(2,1)}), bf16[8,128,128]{2,1,0:T(8,128)(2,1)S(1)}, u32[]{:S(2)}, u32[]{:S(2)}) async-start(bf16[8,128,128]{2,1,0:T(8,128)(2,1)} %get-tuple-element.27), calls=%async_computation.1 | async-start | bytes 524288 | tf_op jit(solution)/shard_map/all_to_all | solution.py:429
  47.2 1.1 %slice_bitcast_fusion.branch = bf16[256,1024]{1,0:T(8,128)(2,1)S(1)} fusion(bf16[3,256,1024]{2,1,0:T(8,128)(2,1)} %branches.1), kind=kLoop, calls=%fused_computation.3 | loop fusion | bytes 1048576 | tf_op jit(solution)/shard_map/squeeze | solution.py:486
  48.2 8.0 %all-to-all-done.1.mixed = bf16[8,128,128]{2,1,0:T(8,128)(2,1)S(1)} async-done(((bf16[8,128,128]{2,1,0:T(8,128)(2,1)}), bf16[8,128,128]{2,1,0:T(8,128)(2,1)S(1)}, u32[]{:S(2)}, u32[]{:S(2)}) %all-to-all-start.1) | async-done | bytes 262176 | tf_op jit(solution)/shard_map/all_to_all | solution.py:429
  56.3 2.6 %gate.2 = (bf16[128,1024]{1,0:T(8,128)(2,1)S(1)}, bf16[128,2048]{1,0:T(8,128)(2,1)S(1)}) custom-call(s32[1]{0:T(128)} %bitcast.place, bf16[8,128,128]{2,1,0:T(8,128)(2,1)S(1)} %all-to-all-done.1.mixed, bf16[256,1024]{1,0:T(8,128)(2,1)S(1)} %slice_bitcast_fusion.branch, f32[3,3,1024]{2,1,0:T(4,128)S(1)} %bitcast.9, bf16[1024,8192]{1,0:T(8,128)(2,1)} %weight.9), custom_call_target="tpu_custom_call" | custom-call | flops 1 | bytes 1 | tf_op jit(solution)/shard_map/gate/pallas_call | solution.py:477
  58.9 0.1 collective-permute-start
  59.0 3.6 %all-to-all-start.2 = ((bf16[8,128,128]{2,1,0:T(8,128)(2,1)}), bf16[8,128,128]{2,1,0:T(8,128)(2,1)S(1)}, u32[]{:S(2)}, u32[]{:S(2)}) async-start(bf16[8,128,128]{2,1,0:T(8,128)(2,1)} %get-tuple-element.29), calls=%async_computation.2 | async-start | bytes 524288 | tf_op jit(solution)/shard_map/all_to_all | solution.py:429
  62.6 2.6 %own.2 = f32[128,2048]{1,0:T(8,128)S(1)} custom-call(s32[1]{0:T(128)} %bitcast.place, bf16[128,1024]{1,0:T(8,128)(2,1)S(1)} %get-tuple-element.35.gated.first, bf16[1024,8192]{1,0:T(8,128)(2,1)} %weight.9), custom_call_target="tpu_custom_call" | custom-call | flops 1 | bytes 1 | tf_op jit(solution)/shard_map/own/pallas_call | solution.py:488
  65.2 0.0 collective-permute-done
  65.2 0.1 add_convert_fusion.2
  65.3 1.6 %collective-permute-start.1 = (bf16[128,2048]{1,0:T(8,128)(2,1)S(1)}, bf16[128,2048]{1,0:T(8,128)(2,1)S(1)}, u32[]{:S(2)}, u32[]{:S(2)}) collective-permute-start(bf16[128,2048]{1,0:T(8,128)(2,1)S(1)} %add_convert_fusion.2), channel_id=1, source_target_pairs={{0,2},{1,3},{2,0},{3,1},{4,6},{5,7},{6,4},{7,5},{8,10},{9,11},{10,... | collective-permute-start | bytes 1572872 | tf_op jit(solution)/shard_map/ppermute | solution.py:426
  66.9 5.3 %all-to-all-done.2.mixed = bf16[8,128,128]{2,1,0:T(8,128)(2,1)S(1)} async-done(((bf16[8,128,128]{2,1,0:T(8,128)(2,1)}), bf16[8,128,128]{2,1,0:T(8,128)(2,1)S(1)}, u32[]{:S(2)}, u32[]{:S(2)}) %all-to-all-start.2) | async-done | bytes 262176 | tf_op jit(solution)/shard_map/all_to_all | solution.py:429
  72.2 2.6 %gate.3 = (bf16[128,1024]{1,0:T(8,128)(2,1)S(1)}, bf16[128,2048]{1,0:T(8,128)(2,1)S(1)}) custom-call(s32[1]{0:T(128)} %bitcast.place, bf16[8,128,128]{2,1,0:T(8,128)(2,1)S(1)} %all-to-all-done.2.mixed, bf16[256,1024]{1,0:T(8,128)(2,1)S(1)} %slice_bitcast_fusion.branch, f32[3,3,1024]{2,1,0:T(4,128)S(1)} %bitcast.10, bf16[1024,8192]{1,0:T(8,128)(2,1)} %weight.9), custom_call_target="tpu_custom_call" | custom-call | flops 1 | bytes 1 | tf_op jit(solution)/shard_map/gate/pallas_call | solution.py:477
  74.8 0.1 collective-permute-start.2
  74.9 2.6 %own.3 = f32[128,2048]{1,0:T(8,128)S(1)} custom-call(s32[1]{0:T(128)} %bitcast.place, bf16[128,1024]{1,0:T(8,128)(2,1)S(1)} %get-tuple-element.36.gated.second, bf16[1024,8192]{1,0:T(8,128)(2,1)} %weight.9), custom_call_target="tpu_custom_call" | custom-call | flops 1 | bytes 1 | tf_op jit(solution)/shard_map/own/pallas_call | solution.py:488
  77.5 2.0 %collective-permute-done.1 = bf16[128,2048]{1,0:T(8,128)(2,1)S(1)} collective-permute-done((bf16[128,2048]{1,0:T(8,128)(2,1)S(1)}, bf16[128,2048]{1,0:T(8,128)(2,1)S(1)}, u32[]{:S(2)}, u32[]{:S(2)}) %collective-permute-start.1) | collective-permute-done | bytes 524320 | tf_op jit(solution)/shard_map/ppermute | solution.py:426
  79.5 0.0 collective-permute-done.2
  79.5 0.1 add_convert_fusion.1
  79.6 1.6 %collective-permute-start.7 = (bf16[128,2048]{1,0:T(8,128)(2,1)S(1)}, bf16[128,2048]{1,0:T(8,128)(2,1)S(1)}, u32[]{:S(2)}, u32[]{:S(2)}) collective-permute-start(bf16[128,2048]{1,0:T(8,128)(2,1)S(1)} %add_convert_fusion.1), channel_id=1, source_target_pairs={{0,2},{1,3},{2,0},{3,1},{4,6},{5,7},{6,4},{7,5},{8,10},{9,11},{10,... | collective-permute-start | bytes 1572872 | tf_op jit(solution)/shard_map/ppermute | solution.py:426
  81.2 4.2 %near.1 = (bf16[256,512]{1,0:T(8,128)(2,1)S(1)}, bf16[256,512]{1,0:T(8,128)(2,1)S(1)}, bf16[256,512]{1,0:T(8,128)(2,1)S(1)}, bf16[256,512]{1,0:T(8,128)(2,1)S(1)}, f32[256,2048]{1,0:T(8,128)S(1)}) custom-call(s32[1]{0:T(128)} %bitcast.place, bf16[128,1024]{1,0:T(8,128)(2,1)S(1)} %get-tuple-element.35.gated.first, ...), custom_call_target="tpu_custom_call" | custom-call | flops 1 | bytes 1 | tf_op jit(solution)/shard_map/near/pallas_call | solution.py:506
  85.4 0.1 collective-permute-start.3
  85.5 0.5 collective-permute-start.4
  86.0 0.1 collective-permute-start.5
  86.1 0.4 collective-permute-start.6
  86.5 0.5 collective-permute-done.3
  87.0 0.4 collective-permute-done.4
  87.4 0.4 collective-permute-done.5
  87.8 0.4 collective-permute-done.6
  88.1 4.9 %collective-permute-done.7 = bf16[128,2048]{1,0:T(8,128)(2,1)S(1)} collective-permute-done((bf16[128,2048]{1,0:T(8,128)(2,1)S(1)}, bf16[128,2048]{1,0:T(8,128)(2,1)S(1)}, u32[]{:S(2)}, u32[]{:S(2)}) %collective-permute-start.7) | collective-permute-done | bytes 524320 | tf_op jit(solution)/shard_map/ppermute | solution.py:426
  93.0 1.4 %add_convert_fusion = bf16[256,2048]{1,0:T(8,128)(2,1)} fusion(f32[256,2048]{1,0:T(8,128)S(1)} %get-tuple-element.37, bf16[256,512]{1,0:T(8,128)(2,1)S(1)} %collective-permute-done.6, bf16[256,512]{1,0:T(8,128)(2,1)S(1)} %collective-permute-done.5, bf16[256,512]{1,0:T(8,128)(2,1)S(1)} %collective-permute-done.4, ...), kind=kLoop, calls=%fused_computation | loop fusion | flops 7864320 | bytes 5242880 | tf_op jit(solution)/shard_map/convert_element_type | solution.py:524
  (1 shorter events, 0.0 us)
Async XLA Ops:
  0.0 10.4 %copy-start = (f32[1024]{0:T(1024)S(1)}, f32[1024]{0:T(1024)}, u32[]{:S(2)}) copy-start(f32[1024]{0:T(1024)} %param.10) | copy-start | bytes 12292
  0.0 10.5 %copy-start.1 = (f32[3,1024,3]{1,2,0:T(4,128)S(1)}, f32[3,1024,3]{1,2,0:T(4,128)}, u32[]{:S(2)}) copy-start(f32[3,1024,3]{1,2,0:T(4,128)} %param.8) | copy-start | bytes 110596
  0.0 36.9 %copy-start.2 = (f32[256,32]{1,0:T(8,128)S(1)}, f32[256,32]{1,0:T(8,128)}, u32[]{:S(2)}) copy-start(f32[256,32]{1,0:T(8,128)} %constant.20.clone.twist) | copy-start | bytes 98308
  0.0 36.9 %copy-start.3 = (bf16[512,512]{1,0:T(8,128)(2,1)S(1)}, bf16[512,512]{1,0:T(8,128)(2,1)}, u32[]{:S(2)}) copy-start(bf16[512,512]{1,0:T(8,128)(2,1)} %constant.19.clone.matrix) | copy-start | bytes 1572868
  3.1 33.7 %all-to-all-start = ((bf16[8,528,128]{2,1,0:T(8,128)(2,1)}), bf16[8,528,128]{2,1,0:T(8,128)(2,1)S(1)}, u32[]{:S(2)}, u32[]{:S(2)}) async-start(bf16[8,528,128]{2,1,0:T(8,128)(2,1)} %product.1), calls=%async_computation | async-start | bytes 2162688 | tf_op jit(solution)/shard_map/all_to_all | solution.py:429
  43.6 12.7 %all-to-all-start.1 = ((bf16[8,128,128]{2,1,0:T(8,128)(2,1)}), bf16[8,128,128]{2,1,0:T(8,128)(2,1)S(1)}, u32[]{:S(2)}, u32[]{:S(2)}) async-start(bf16[8,128,128]{2,1,0:T(8,128)(2,1)} %get-tuple-element.27), calls=%async_computation.1 | async-start | bytes 524288 | tf_op jit(solution)/shard_map/all_to_all | solution.py:429
  58.9 6.3 %collective-permute-start = (bf16[128,2048]{1,0:T(8,128)(2,1)S(1)}, bf16[128,2048]{1,0:T(8,128)(2,1)S(1)}, u32[]{:S(2)}, u32[]{:S(2)}) collective-permute-start(bf16[128,2048]{1,0:T(8,128)(2,1)S(1)} %get-tuple-element.30), channel_id=1, source_target_pairs={{0,1},{1,0},{2,3},{3,2},{4,5},{5,4},{6,7},{7,6},{8,9},{9,8},{10,11... | collective-permute-start | bytes 1572872 | tf_op jit(solution)/shard_map/ppermute | solution.py:426
  59.0 13.2 %all-to-all-start.2 = ((bf16[8,128,128]{2,1,0:T(8,128)(2,1)}), bf16[8,128,128]{2,1,0:T(8,128)(2,1)S(1)}, u32[]{:S(2)}, u32[]{:S(2)}) async-start(bf16[8,128,128]{2,1,0:T(8,128)(2,1)} %get-tuple-element.29), calls=%async_computation.2 | async-start | bytes 524288 | tf_op jit(solution)/shard_map/all_to_all | solution.py:429
  65.3 14.2 %collective-permute-start.1 = (bf16[128,2048]{1,0:T(8,128)(2,1)S(1)}, bf16[128,2048]{1,0:T(8,128)(2,1)S(1)}, u32[]{:S(2)}, u32[]{:S(2)}) collective-permute-start(bf16[128,2048]{1,0:T(8,128)(2,1)S(1)} %add_convert_fusion.2), channel_id=1, source_target_pairs={{0,2},{1,3},{2,0},{3,1},{4,6},{5,7},{6,4},{7,5},{8,10},{9,11},{10,... | collective-permute-start | bytes 1572872 | tf_op jit(solution)/shard_map/ppermute | solution.py:426
  74.8 4.7 %collective-permute-start.2 = (bf16[128,2048]{1,0:T(8,128)(2,1)S(1)}, bf16[128,2048]{1,0:T(8,128)(2,1)S(1)}, u32[]{:S(2)}, u32[]{:S(2)}) collective-permute-start(bf16[128,2048]{1,0:T(8,128)(2,1)S(1)} %get-tuple-element.34), channel_id=1, source_target_pairs={{0,1},{1,0},{2,3},{3,2},{4,5},{5,4},{6,7},{7,6},{8,9},{9,8},{10,11... | collective-permute-start | bytes 1572872 | tf_op jit(solution)/shard_map/ppermute | solution.py:426
  79.6 13.4 %collective-permute-start.7 = (bf16[128,2048]{1,0:T(8,128)(2,1)S(1)}, bf16[128,2048]{1,0:T(8,128)(2,1)S(1)}, u32[]{:S(2)}, u32[]{:S(2)}) collective-permute-start(bf16[128,2048]{1,0:T(8,128)(2,1)S(1)} %add_convert_fusion.1), channel_id=1, source_target_pairs={{0,2},{1,3},{2,0},{3,1},{4,6},{5,7},{6,4},{7,5},{8,10},{9,11},{10,... | collective-permute-start | bytes 1572872 | tf_op jit(solution)/shard_map/ppermute | solution.py:426
  85.4 1.6 %collective-permute-start.3 = (bf16[256,512]{1,0:T(8,128)(2,1)S(1)}, bf16[256,512]{1,0:T(8,128)(2,1)S(1)}, u32[]{:S(2)}, u32[]{:S(2)}) collective-permute-start(bf16[256,512]{1,0:T(8,128)(2,1)S(1)} %get-tuple-element.38), channel_id=1, source_target_pairs={{0,1},{1,0},{2,3},{3,2},{4,5},{5,4},{6,7},{7,6},{8,9},{9,8},{10,11... | collective-permute-start | bytes 786440 | tf_op jit(solution)/shard_map/ppermute | solution.py:426
  85.5 1.9 %collective-permute-start.4 = (bf16[256,512]{1,0:T(8,128)(2,1)S(1)}, bf16[256,512]{1,0:T(8,128)(2,1)S(1)}, u32[]{:S(2)}, u32[]{:S(2)}) collective-permute-start(bf16[256,512]{1,0:T(8,128)(2,1)S(1)} %get-tuple-element.39), channel_id=1, source_target_pairs={{0,1},{1,0},{2,3},{3,2},{4,5},{5,4},{6,7},{7,6},{8,9},{9,8},{10,11... | collective-permute-start | bytes 786440 | tf_op jit(solution)/shard_map/ppermute | solution.py:426
  86.0 1.8 %collective-permute-start.5 = (bf16[256,512]{1,0:T(8,128)(2,1)S(1)}, bf16[256,512]{1,0:T(8,128)(2,1)S(1)}, u32[]{:S(2)}, u32[]{:S(2)}) collective-permute-start(bf16[256,512]{1,0:T(8,128)(2,1)S(1)} %get-tuple-element.40), channel_id=1, source_target_pairs={{0,1},{1,0},{2,3},{3,2},{4,5},{5,4},{6,7},{7,6},{8,9},{9,8},{10,11... | collective-permute-start | bytes 786440 | tf_op jit(solution)/shard_map/ppermute | solution.py:426
  86.1 2.1 %collective-permute-start.6 = (bf16[256,512]{1,0:T(8,128)(2,1)S(1)}, bf16[256,512]{1,0:T(8,128)(2,1)S(1)}, u32[]{:S(2)}, u32[]{:S(2)}) collective-permute-start(bf16[256,512]{1,0:T(8,128)(2,1)S(1)} %get-tuple-element.41), channel_id=1, source_target_pairs={{0,1},{1,0},{2,3},{3,2},{4,5},{5,4},{6,7},{7,6},{8,9},{9,8},{10,11... | collective-permute-start | bytes 786440 | tf_op jit(solution)/shard_map/ppermute | solution.py:426

commit v3 on v2

--- a/solution.py
+++ b/solution.py
@@ -452,7 +452,7 @@
         cost_estimate=cost(seq_count * 12 * (2 * tokens) ** 2 * width, 6 << 20),
         name="transform",
     )(matrix, twist, my_taps, signals)
-    counts = (tokens * 128 // 256, tokens * 128 // 256)
+    counts = (tokens * 176 // 256, tokens * 80 // 256)
     mixed = pl.pallas_call(
         back_kernel,
         in_specs=[VMEM] * 5,
@@ -462,7 +462,6 @@
         cost_estimate=cost(200 * tokens * channels, 5 << 20),
         name="back",
     )(twist, gain, gates, turned, product)
-    mixed = [across(part) for part in mixed]
 
     flops, moved = 2 * tokens * channels * features, 2 * channels * features
     held = pltpu.VMEM((2, channels, features), BF16)
@@ -474,6 +473,7 @@
         total = pltpu.VMEM((count, features), F32)
         if step:
             value, sent = lax.optimization_barrier((value, sent))
+        value = across(value)
         ready, part = pl.pallas_call(
             functools.partial(gate_kernel, start),
             in_specs=[SMEM] + [VMEM] * 3 + [HBM],

time: 94.9 us -> 94.2 us (level)
  blocking collectives: 0 us -> 11.3 us
  waiting for transfers between devices: 48.2 us -> 39.8 us
  starting transfers between devices: 18.9 us -> 15.2 us
    all_to_all x0 -> x1, blocking collectives: none -> 11.3 us  [across(): return lax.all_to_all(value, 'seq', 0, 0, tiled=True)]
    ppermute x8, waiting for transfers between devices: 8.54 us -> 3.32 us  [exchanged(): return lax.ppermute(value, 'mp', [(m, m ^ bit) for m in range(mp_count)])]
    all_to_all x3 -> x2, starting transfers between devices: 14.5 us -> 10.9 us  [across(): return lax.all_to_all(value, 'seq', 0, 0, tiled=True)]
    all_to_all x3 -> x2, waiting for transfers between devices: 39.7 us -> 36.5 us  [across(): return lax.all_to_all(value, 'seq', 0, 0, tiled=True)]
  transfers between devices with their start and end apart: 11 -> 10, of which waited for: 9 -> 8; matrix products, arithmetic and copies ran while one was open for 1% -> 1% of each run, Pallas kernels for 13% -> 13%
where the time goes in v3:
time: 94.2 us; the launch traced here: 93.8 us
  waiting for transfers between devices  39.8 us (42%)
  Pallas kernels  24.6 us (26%)
  starting transfers between devices  15.2 us (16%)
  blocking collectives  11.3 us (12%)
  other arithmetic  1.63 us (2%)
  local copies, waits for them, and re-layouts  1.17 us (1%)
    all_to_all x2, waiting for transfers between devices, across(): return lax.all_to_all(value, 'seq', 0, 0, tiled=True)  36.5 us
    all_to_all x1, blocking collectives, across(): return lax.all_to_all(value, 'seq', 0, 0, tiled=True)  11.3 us
    all_to_all x2, starting transfers between devices, across(): return lax.all_to_all(value, 'seq', 0, 0, tiled=True)  10.9 us
    pallas_call x2, Pallas kernels, shards(): pl.pallas_call(functools.partial(gate_kernel, start), in_specs=[SMEM] + [...  5.29 us
    pallas_call x2, Pallas kernels, shards(): pl.pallas_call(own_kernel, in_specs=[SMEM, VMEM, HBM], out_specs=VMEM, ou...  5.29 us
    pallas_call x1, Pallas kernels, shards(): pl.pallas_call(transform_kernel, in_specs=[VMEM] * 4, out_specs=[VMEM] *...  4.63 us
    ppermute x8, starting transfers between devices, exchanged(): return lax.ppermute(value, 'mp', [(m, m ^ bit) for m in range(mp_count)])  4.38 us
    pallas_call x1, Pallas kernels, shards(): pl.pallas_call(near_kernel, in_specs=[SMEM, VMEM, VMEM, HBM], out_specs=[...  4.19 us
  transfers between devices with their start and end apart: 10, of which 8 were waited for; matrix products, arithmetic and copies ran while one was open for 1% of the time, Pallas kernels for 13%

profile of v3, /device:TPU:0, one launch (start us, length us, event | category | flops | bytes accessed | tf_op | source)
XLA Modules:
  0.0 93.8 jit_solution(11703166465484786576)
XLA Ops:
  0.0 0.0 copy-start
  0.0 0.0 copy-start.1
  0.0 0.0 copy-start.2
  0.0 0.0 copy-start.3
  0.0 3.1 %product.1 = bf16[8,528,128]{2,1,0:T(8,128)(2,1)} custom-call(f32[3,3,1024]{2,1,0:T(4,128)} %bitcast.8, bf16[3,256,1024]{2,1,0:T(8,128)(2,1)} %branches.1, bf16[256,1024]{1,0:T(8,128)(2,1)} %filt.1), custom_call_target="tpu_custom_call" | custom-call | flops 10485760 | bytes 2621440 | tf_op jit(solution)/shard_map/product/pallas_call | solution.py:179
  3.1 7.3 %all-to-all-start = ((bf16[8,528,128]{2,1,0:T(8,128)(2,1)}), bf16[8,528,128]{2,1,0:T(8,128)(2,1)S(1)}, u32[]{:S(2)}, u32[]{:S(2)}) async-start(bf16[8,528,128]{2,1,0:T(8,128)(2,1)} %product.1), calls=%async_computation | async-start | bytes 2162688 | tf_op jit(solution)/shard_map/all_to_all | solution.py:429
  10.4 0.0 copy-done
  10.4 0.1 dynamic-slice_bitcast_fusion.1.gain
  10.5 0.0 copy-done.1
  10.5 26.4 %all-to-all-done.signals = bf16[8,528,128]{2,1,0:T(8,128)(2,1)S(1)} async-done(((bf16[8,528,128]{2,1,0:T(8,128)(2,1)}), bf16[8,528,128]{2,1,0:T(8,128)(2,1)S(1)}, u32[]{:S(2)}, u32[]{:S(2)}) %all-to-all-start) | async-done | bytes 1081376 | tf_op jit(solution)/shard_map/all_to_all | solution.py:429
  36.9 0.0 copy-done.2
  36.9 0.0 copy-done.3
  36.9 4.6 %transform.1 = (f32[5,512,256]{2,1,0:T(8,128)S(1)}, bf16[8,256,128]{2,1,0:T(8,128)(2,1)S(1)}, f32[8,16,128]{2,1,0:T(8,128)S(1)}) custom-call(bf16[512,512]{1,0:T(8,128)(2,1)S(1)} %copy-done.3, f32[256,32]{1,0:T(8,128)S(1)} %copy-done.2, f32[3,3,128]{2,1,0:T(4,128)S(1)} %dynamic-slice_bitcast_fusion.taps, bf16[8,528,128]{2,1,0:T(8,128)(2,1)S(1)} %all-to-all-done.signals), custom_call_target="tpu_custom_call" | custom-call | flops 3221225472 | bytes 6291456 | tf_op jit(solution)/shard_map/transform/pallas_call | solution.py:441
  41.5 2.1 %back.1 = (bf16[8,176,128]{2,1,0:T(8,128)(2,1)}, bf16[8,80,128]{2,1,0:T(8,128)(2,1)S(1)}) custom-call(f32[256,32]{1,0:T(8,128)S(1)} %copy-done.2, f32[1,128]{1,0:T(1,128)S(1)} %dynamic-slice_bitcast_fusion.1.gain, f32[8,16,128]{2,1,0:T(8,128)S(1)} %get-tuple-element.24.gates, f32[5,512,256]{2,1,0:T(8,128)S(1)} %get-tuple-element.25.turned, ...), custom_call_target="tpu_custom_call" | custom-call | flops 52428800 | bytes 5242880 | tf_op jit(solution)/shard_map/back/pallas_call | solution.py:456
  43.6 3.6 %all-to-all-start.1 = ((bf16[8,176,128]{2,1,0:T(8,128)(2,1)}), bf16[8,176,128]{2,1,0:T(8,128)(2,1)S(1)}, u32[]{:S(2)}, u32[]{:S(2)}) async-start(bf16[8,176,128]{2,1,0:T(8,128)(2,1)} %get-tuple-element.27), calls=%async_computation.1 | async-start | bytes 720896 | tf_op jit(solution)/shard_map/all_to_all | solution.py:429
  47.2 1.1 %slice_bitcast_fusion.branch = bf16[256,1024]{1,0:T(8,128)(2,1)S(1)} fusion(bf16[3,256,1024]{2,1,0:T(8,128)(2,1)} %branches.1), kind=kLoop, calls=%fused_computation.3 | loop fusion | bytes 1048576 | tf_op jit(solution)/shard_map/squeeze | solution.py:486
  48.3 10.1 %all-to-all-done.1.mixed = bf16[8,176,128]{2,1,0:T(8,128)(2,1)S(1)} async-done(((bf16[8,176,128]{2,1,0:T(8,128)(2,1)}), bf16[8,176,128]{2,1,0:T(8,128)(2,1)S(1)}, u32[]{:S(2)}, u32[]{:S(2)}) %all-to-all-start.1) | async-done | bytes 360480 | tf_op jit(solution)/shard_map/all_to_all | solution.py:429
  58.4 2.7 %gate.2 = (bf16[176,1024]{1,0:T(8,128)(2,1)S(1)}, bf16[176,2048]{1,0:T(8,128)(2,1)S(1)}) custom-call(s32[1]{0:T(128)} %bitcast.place, bf16[8,176,128]{2,1,0:T(8,128)(2,1)S(1)} %all-to-all-done.1.mixed, bf16[256,1024]{1,0:T(8,128)(2,1)S(1)} %slice_bitcast_fusion.branch, f32[3,3,1024]{2,1,0:T(4,128)S(1)} %bitcast.9, bf16[1024,8192]{1,0:T(8,128)(2,1)} %weight.9), custom_call_target="tpu_custom_call" | custom-call | flops 1 | bytes 1 | tf_op jit(solution)/shard_map/gate/pallas_call | solution.py:477
  61.0 0.1 collective-permute-start
  61.1 2.7 %own.2 = f32[176,2048]{1,0:T(8,128)S(1)} custom-call(s32[1]{0:T(128)} %bitcast.place, bf16[176,1024]{1,0:T(8,128)(2,1)S(1)} %get-tuple-element.35.gated.first, bf16[1024,8192]{1,0:T(8,128)(2,1)} %weight.9), custom_call_target="tpu_custom_call" | custom-call | flops 1 | bytes 1 | tf_op jit(solution)/shard_map/own/pallas_call | solution.py:488
  63.8 0.0 collective-permute-done
  63.8 0.2 add_convert_fusion.1
  64.0 1.6 %collective-permute-start.1 = (bf16[176,2048]{1,0:T(8,128)(2,1)S(1)}, bf16[176,2048]{1,0:T(8,128)(2,1)S(1)}, u32[]{:S(2)}, u32[]{:S(2)}) collective-permute-start(bf16[176,2048]{1,0:T(8,128)(2,1)S(1)} %add_convert_fusion.1), channel_id=1, source_target_pairs={{0,2},{1,3},{2,0},{3,1},{4,6},{5,7},{6,4},{7,5},{8,10},{9,11},{10,... | collective-permute-start | bytes 2162696 | tf_op jit(solution)/shard_map/ppermute | solution.py:426
  65.6 11.3 %all_to_all.15.mixed = bf16[8,80,128]{2,1,0:T(8,128)(2,1)S(1)} all-to-all(bf16[8,80,128]{2,1,0:T(8,128)(2,1)S(1)} %get-tuple-element.31), channel_id=1, replica_groups=mesh['seq'=8,'mp'=4] {'seq'}, dimensions={0} | all-to-all | bytes 327680 | tf_op jit(solution)/shard_map/all_to_all | solution.py:429
  76.8 2.6 %gate.3 = (bf16[80,1024]{1,0:T(8,128)(2,1)S(1)}, bf16[80,2048]{1,0:T(8,128)(2,1)S(1)}) custom-call(s32[1]{0:T(128)} %bitcast.place, bf16[8,80,128]{2,1,0:T(8,128)(2,1)S(1)} %all_to_all.15.mixed, bf16[256,1024]{1,0:T(8,128)(2,1)S(1)} %slice_bitcast_fusion.branch, f32[3,3,1024]{2,1,0:T(4,128)S(1)} %bitcast.10, bf16[1024,8192]{1,0:T(8,128)(2,1)} %weight.9), custom_call_target="tpu_custom_call" | custom-call | flops 1 | bytes 1 | tf_op jit(solution)/shard_map/gate/pallas_call | solution.py:477
  79.4 0.1 collective-permute-start.2
  79.5 2.6 %own.3 = f32[80,2048]{1,0:T(8,128)S(1)} custom-call(s32[1]{0:T(128)} %bitcast.place, bf16[80,1024]{1,0:T(8,128)(2,1)S(1)} %get-tuple-element.36.gated.second, bf16[1024,8192]{1,0:T(8,128)(2,1)} %weight.9), custom_call_target="tpu_custom_call" | custom-call | flops 1 | bytes 1 | tf_op jit(solution)/shard_map/own/pallas_call | solution.py:488
  82.1 0.4 collective-permute-done.1
  82.6 0.0 collective-permute-done.2
  82.6 0.1 add_convert_fusion.2
  82.6 1.6 %collective-permute-start.7 = (bf16[80,2048]{1,0:T(8,128)(2,1)S(1)}, bf16[80,2048]{1,0:T(8,128)(2,1)S(1)}, u32[]{:S(2)}, u32[]{:S(2)}) collective-permute-start(bf16[80,2048]{1,0:T(8,128)(2,1)S(1)} %add_convert_fusion.2), channel_id=1, source_target_pairs={{0,2},{1,3},{2,0},{3,1},{4,6},{5,7},{6,4},{7,5},{8,10},{9,11},{10,... | collective-permute-start | bytes 983048 | tf_op jit(solution)/shard_map/ppermute | solution.py:426
  84.2 4.2 %near.1 = (bf16[256,512]{1,0:T(8,128)(2,1)S(1)}, bf16[256,512]{1,0:T(8,128)(2,1)S(1)}, bf16[256,512]{1,0:T(8,128)(2,1)S(1)}, bf16[256,512]{1,0:T(8,128)(2,1)S(1)}, f32[256,2048]{1,0:T(8,128)S(1)}) custom-call(s32[1]{0:T(128)} %bitcast.place, bf16[176,1024]{1,0:T(8,128)(2,1)S(1)} %get-tuple-element.35.gated.first, ...), custom_call_target="tpu_custom_call" | custom-call | flops 1 | bytes 1 | tf_op jit(solution)/shard_map/near/pallas_call | solution.py:506
  88.4 0.1 collective-permute-start.3
  88.5 0.5 collective-permute-start.4
  89.0 0.1 collective-permute-start.5
  89.1 0.4 collective-permute-start.6
  89.5 0.5 collective-permute-done.3
  90.0 0.4 collective-permute-done.4
  90.4 0.4 collective-permute-done.5
  90.8 0.4 collective-permute-done.6
  91.1 1.3 %collective-permute-done.7 = bf16[80,2048]{1,0:T(8,128)(2,1)S(1)} collective-permute-done((bf16[80,2048]{1,0:T(8,128)(2,1)S(1)}, bf16[80,2048]{1,0:T(8,128)(2,1)S(1)}, u32[]{:S(2)}, u32[]{:S(2)}) %collective-permute-start.7) | collective-permute-done | bytes 327712 | tf_op jit(solution)/shard_map/ppermute | solution.py:426
  92.4 1.4 %add_convert_fusion = bf16[256,2048]{1,0:T(8,128)(2,1)} fusion(f32[256,2048]{1,0:T(8,128)S(1)} %get-tuple-element.37, bf16[256,512]{1,0:T(8,128)(2,1)S(1)} %collective-permute-done.6, bf16[256,512]{1,0:T(8,128)(2,1)S(1)} %collective-permute-done.5, bf16[256,512]{1,0:T(8,128)(2,1)S(1)} %collective-permute-done.4, ...), kind=kLoop, calls=%fused_computation | loop fusion | flops 7864320 | bytes 5242880 | tf_op jit(solution)/shard_map/convert_element_type | solution.py:524
  (1 shorter events, 0.0 us)
Async XLA Ops:
  0.0 10.4 %copy-start = (f32[1024]{0:T(1024)S(1)}, f32[1024]{0:T(1024)}, u32[]{:S(2)}) copy-start(f32[1024]{0:T(1024)} %param.10) | copy-start | bytes 12292
  0.0 10.5 %copy-start.1 = (f32[3,1024,3]{1,2,0:T(4,128)S(1)}, f32[3,1024,3]{1,2,0:T(4,128)}, u32[]{:S(2)}) copy-start(f32[3,1024,3]{1,2,0:T(4,128)} %param.8) | copy-start | bytes 110596
  0.0 36.9 %copy-start.2 = (f32[256,32]{1,0:T(8,128)S(1)}, f32[256,32]{1,0:T(8,128)}, u32[]{:S(2)}) copy-start(f32[256,32]{1,0:T(8,128)} %constant.20.clone.twist) | copy-start | bytes 98308
  0.0 36.9 %copy-start.3 = (bf16[512,512]{1,0:T(8,128)(2,1)S(1)}, bf16[512,512]{1,0:T(8,128)(2,1)}, u32[]{:S(2)}) copy-start(bf16[512,512]{1,0:T(8,128)(2,1)} %constant.19.clone.matrix) | copy-start | bytes 1572868
  3.1 33.7 %all-to-all-start = ((bf16[8,528,128]{2,1,0:T(8,128)(2,1)}), bf16[8,528,128]{2,1,0:T(8,128)(2,1)S(1)}, u32[]{:S(2)}, u32[]{:S(2)}) async-start(bf16[8,528,128]{2,1,0:T(8,128)(2,1)} %product.1), calls=%async_computation | async-start | bytes 2162688 | tf_op jit(solution)/shard_map/all_to_all | solution.py:429
  43.6 14.8 %all-to-all-start.1 = ((bf16[8,176,128]{2,1,0:T(8,128)(2,1)}), bf16[8,176,128]{2,1,0:T(8,128)(2,1)S(1)}, u32[]{:S(2)}, u32[]{:S(2)}) async-start(bf16[8,176,128]{2,1,0:T(8,128)(2,1)} %get-tuple-element.27), calls=%async_computation.1 | async-start | bytes 720896 | tf_op jit(solution)/shard_map/all_to_all | solution.py:429
  61.0 2.8 %collective-permute-start = (bf16[176,2048]{1,0:T(8,128)(2,1)S(1)}, bf16[176,2048]{1,0:T(8,128)(2,1)S(1)}, u32[]{:S(2)}, u32[]{:S(2)}) collective-permute-start(bf16[176,2048]{1,0:T(8,128)(2,1)S(1)} %get-tuple-element.30), channel_id=1, source_target_pairs={{0,1},{1,0},{2,3},{3,2},{4,5},{5,4},{6,7},{7,6},{8,9},{9,8},{10,11... | collective-permute-start | bytes 2162696 | tf_op jit(solution)/shard_map/ppermute | solution.py:426
  64.0 18.6 %collective-permute-start.1 = (bf16[176,2048]{1,0:T(8,128)(2,1)S(1)}, bf16[176,2048]{1,0:T(8,128)(2,1)S(1)}, u32[]{:S(2)}, u32[]{:S(2)}) collective-permute-start(bf16[176,2048]{1,0:T(8,128)(2,1)S(1)} %add_convert_fusion.1), channel_id=1, source_target_pairs={{0,2},{1,3},{2,0},{3,1},{4,6},{5,7},{6,4},{7,5},{8,10},{9,11},{10,... | collective-permute-start | bytes 2162696 | tf_op jit(solution)/shard_map/ppermute | solution.py:426
  79.4 3.1 %collective-permute-start.2 = (bf16[80,2048]{1,0:T(8,128)(2,1)S(1)}, bf16[80,2048]{1,0:T(8,128)(2,1)S(1)}, u32[]{:S(2)}, u32[]{:S(2)}) collective-permute-start(bf16[80,2048]{1,0:T(8,128)(2,1)S(1)} %get-tuple-element.34), channel_id=1, source_target_pairs={{0,1},{1,0},{2,3},{3,2},{4,5},{5,4},{6,7},{7,6},{8,9},{9,8},{10,11... | collective-permute-start | bytes 983048 | tf_op jit(solution)/shard_map/ppermute | solution.py:426
  82.6 9.8 %collective-permute-start.7 = (bf16[80,2048]{1,0:T(8,128)(2,1)S(1)}, bf16[80,2048]{1,0:T(8,128)(2,1)S(1)}, u32[]{:S(2)}, u32[]{:S(2)}) collective-permute-start(bf16[80,2048]{1,0:T(8,128)(2,1)S(1)} %add_convert_fusion.2), channel_id=1, source_target_pairs={{0,2},{1,3},{2,0},{3,1},{4,6},{5,7},{6,4},{7,5},{8,10},{9,11},{10,... | collective-permute-start | bytes 983048 | tf_op jit(solution)/shard_map/ppermute | solution.py:426
  88.4 1.6 %collective-permute-start.3 = (bf16[256,512]{1,0:T(8,128)(2,1)S(1)}, bf16[256,512]{1,0:T(8,128)(2,1)S(1)}, u32[]{:S(2)}, u32[]{:S(2)}) collective-permute-start(bf16[256,512]{1,0:T(8,128)(2,1)S(1)} %get-tuple-element.38), channel_id=1, source_target_pairs={{0,1},{1,0},{2,3},{3,2},{4,5},{5,4},{6,7},{7,6},{8,9},{9,8},{10,11... | collective-permute-start | bytes 786440 | tf_op jit(solution)/shard_map/ppermute | solution.py:426
  88.5 1.9 %collective-permute-start.4 = (bf16[256,512]{1,0:T(8,128)(2,1)S(1)}, bf16[256,512]{1,0:T(8,128)(2,1)S(1)}, u32[]{:S(2)}, u32[]{:S(2)}) collective-permute-start(bf16[256,512]{1,0:T(8,128)(2,1)S(1)} %get-tuple-element.39), channel_id=1, source_target_pairs={{0,1},{1,0},{2,3},{3,2},{4,5},{5,4},{6,7},{7,6},{8,9},{9,8},{10,11... | collective-permute-start | bytes 786440 | tf_op jit(solution)/shard_map/ppermute | solution.py:426
  89.0 1.8 %collective-permute-start.5 = (bf16[256,512]{1,0:T(8,128)(2,1)S(1)}, bf16[256,512]{1,0:T(8,128)(2,1)S(1)}, u32[]{:S(2)}, u32[]{:S(2)}) collective-permute-start(bf16[256,512]{1,0:T(8,128)(2,1)S(1)} %get-tuple-element.40), channel_id=1, source_target_pairs={{0,1},{1,0},{2,3},{3,2},{4,5},{5,4},{6,7},{7,6},{8,9},{9,8},{10,11... | collective-permute-start | bytes 786440 | tf_op jit(solution)/shard_map/ppermute | solution.py:426
  89.1 2.1 %collective-permute-start.6 = (bf16[256,512]{1,0:T(8,128)(2,1)S(1)}, bf16[256,512]{1,0:T(8,128)(2,1)S(1)}, u32[]{:S(2)}, u32[]{:S(2)}) collective-permute-start(bf16[256,512]{1,0:T(8,128)(2,1)S(1)} %get-tuple-element.41), channel_id=1, source_target_pairs={{0,1},{1,0},{2,3},{3,2},{4,5},{5,4},{6,7},{7,6},{8,9},{9,8},{10,11... | collective-permute-start | bytes 786440 | tf_op jit(solution)/shard_map/ppermute | solution.py:426

commit v4 on v3

--- a/solution.py
+++ b/solution.py
@@ -98,7 +98,7 @@
 SMEM = pl.BlockSpec(memory_space=pltpu.SMEM)
 HBM = pl.BlockSpec(memory_space=pltpu.HBM)
 TILE = 512
-PIECES = 8
+PIECES = 4
 STEPS = 4
 BRANCHES = 3
 

time: 94.2 us -> 94 us (level)
  no operation moved by 1% of the time
where the time goes in v4:
time: 94 us; the launch traced here: 93.6 us
  waiting for transfers between devices  39.9 us (42%)
  Pallas kernels  24.3 us (26%)
  starting transfers between devices  15.3 us (16%)
  blocking collectives  11.2 us (12%)
  other arithmetic  1.63 us (2%)
  local copies, waits for them, and re-layouts  1.17 us (1%)
    all_to_all x2, waiting for transfers between devices, across(): return lax.all_to_all(value, 'seq', 0, 0, tiled=True)  36.5 us
    all_to_all x1, blocking collectives, across(): return lax.all_to_all(value, 'seq', 0, 0, tiled=True)  11.2 us
    all_to_all x2, starting transfers between devices, across(): return lax.all_to_all(value, 'seq', 0, 0, tiled=True)  10.9 us
    pallas_call x2, Pallas kernels, shards(): pl.pallas_call(functools.partial(gate_kernel, start), in_specs=[SMEM] + [...  5.2 us
    pallas_call x2, Pallas kernels, shards(): pl.pallas_call(own_kernel, in_specs=[SMEM, VMEM, HBM], out_specs=VMEM, ou...  5.18 us
    pallas_call x1, Pallas kernels, shards(): pl.pallas_call(transform_kernel, in_specs=[VMEM] * 4, out_specs=[VMEM] *...  4.63 us
    ppermute x8, starting transfers between devices, exchanged(): return lax.ppermute(value, 'mp', [(m, m ^ bit) for m in range(mp_count)])  4.4 us
    pallas_call x1, Pallas kernels, shards(): pl.pallas_call(near_kernel, in_specs=[SMEM, VMEM, VMEM, HBM], out_specs=[...  4.13 us
  transfers between devices with their start and end apart: 10, of which 8 were waited for; matrix products, arithmetic and copies ran while one was open for 1% of the time, Pallas kernels for 13%

profile of v4, /device:TPU:0, one launch (start us, length us, event | category | flops | bytes accessed | tf_op | source)
XLA Modules:
  0.0 93.6 jit_solution(5111509989820006171)
XLA Ops:
  0.0 0.0 copy-start
  0.0 0.0 copy-start.1
  0.0 0.0 copy-start.2
  0.0 0.0 copy-start.3
  0.0 3.1 %product.1 = bf16[8,528,128]{2,1,0:T(8,128)(2,1)} custom-call(f32[3,3,1024]{2,1,0:T(4,128)} %bitcast.8, bf16[3,256,1024]{2,1,0:T(8,128)(2,1)} %branches.1, bf16[256,1024]{1,0:T(8,128)(2,1)} %filt.1), custom_call_target="tpu_custom_call" | custom-call | flops 10485760 | bytes 2621440 | tf_op jit(solution)/shard_map/product/pallas_call | solution.py:179
  3.1 7.3 %all-to-all-start = ((bf16[8,528,128]{2,1,0:T(8,128)(2,1)}), bf16[8,528,128]{2,1,0:T(8,128)(2,1)S(1)}, u32[]{:S(2)}, u32[]{:S(2)}) async-start(bf16[8,528,128]{2,1,0:T(8,128)(2,1)} %product.1), calls=%async_computation | async-start | bytes 2162688 | tf_op jit(solution)/shard_map/all_to_all | solution.py:429
  10.4 0.0 copy-done
  10.4 0.1 dynamic-slice_bitcast_fusion.1.gain
  10.5 0.0 copy-done.1
  10.5 26.4 %all-to-all-done.signals = bf16[8,528,128]{2,1,0:T(8,128)(2,1)S(1)} async-done(((bf16[8,528,128]{2,1,0:T(8,128)(2,1)}), bf16[8,528,128]{2,1,0:T(8,128)(2,1)S(1)}, u32[]{:S(2)}, u32[]{:S(2)}) %all-to-all-start) | async-done | bytes 1081376 | tf_op jit(solution)/shard_map/all_to_all | solution.py:429
  36.9 0.0 copy-done.2
  36.9 0.0 copy-done.3
  36.9 4.6 %transform.1 = (f32[5,512,256]{2,1,0:T(8,128)S(1)}, bf16[8,256,128]{2,1,0:T(8,128)(2,1)S(1)}, f32[8,16,128]{2,1,0:T(8,128)S(1)}) custom-call(bf16[512,512]{1,0:T(8,128)(2,1)S(1)} %copy-done.3, f32[256,32]{1,0:T(8,128)S(1)} %copy-done.2, f32[3,3,128]{2,1,0:T(4,128)S(1)} %dynamic-slice_bitcast_fusion.taps, bf16[8,528,128]{2,1,0:T(8,128)(2,1)S(1)} %all-to-all-done.signals), custom_call_target="tpu_custom_call" | custom-call | flops 3221225472 | bytes 6291456 | tf_op jit(solution)/shard_map/transform/pallas_call | solution.py:441
  41.5 2.1 %back.1 = (bf16[8,176,128]{2,1,0:T(8,128)(2,1)}, bf16[8,80,128]{2,1,0:T(8,128)(2,1)S(1)}) custom-call(f32[256,32]{1,0:T(8,128)S(1)} %copy-done.2, f32[1,128]{1,0:T(1,128)S(1)} %dynamic-slice_bitcast_fusion.1.gain, f32[8,16,128]{2,1,0:T(8,128)S(1)} %get-tuple-element.24.gates, f32[5,512,256]{2,1,0:T(8,128)S(1)} %get-tuple-element.25.turned, ...), custom_call_target="tpu_custom_call" | custom-call | flops 52428800 | bytes 5242880 | tf_op jit(solution)/shard_map/back/pallas_call | solution.py:456
  43.6 3.6 %all-to-all-start.1 = ((bf16[8,176,128]{2,1,0:T(8,128)(2,1)}), bf16[8,176,128]{2,1,0:T(8,128)(2,1)S(1)}, u32[]{:S(2)}, u32[]{:S(2)}) async-start(bf16[8,176,128]{2,1,0:T(8,128)(2,1)} %get-tuple-element.27), calls=%async_computation.1 | async-start | bytes 720896 | tf_op jit(solution)/shard_map/all_to_all | solution.py:429
  47.2 1.1 %slice_bitcast_fusion.branch = bf16[256,1024]{1,0:T(8,128)(2,1)S(1)} fusion(bf16[3,256,1024]{2,1,0:T(8,128)(2,1)} %branches.1), kind=kLoop, calls=%fused_computation.3 | loop fusion | bytes 1048576 | tf_op jit(solution)/shard_map/squeeze | solution.py:486
  48.3 10.1 %all-to-all-done.1.mixed = bf16[8,176,128]{2,1,0:T(8,128)(2,1)S(1)} async-done(((bf16[8,176,128]{2,1,0:T(8,128)(2,1)}), bf16[8,176,128]{2,1,0:T(8,128)(2,1)S(1)}, u32[]{:S(2)}, u32[]{:S(2)}) %all-to-all-start.1) | async-done | bytes 360480 | tf_op jit(solution)/shard_map/all_to_all | solution.py:429
  58.4 2.6 %gate.2 = (bf16[176,1024]{1,0:T(8,128)(2,1)S(1)}, bf16[176,2048]{1,0:T(8,128)(2,1)S(1)}) custom-call(s32[1]{0:T(128)} %bitcast.place, bf16[8,176,128]{2,1,0:T(8,128)(2,1)S(1)} %all-to-all-done.1.mixed, bf16[256,1024]{1,0:T(8,128)(2,1)S(1)} %slice_bitcast_fusion.branch, f32[3,3,1024]{2,1,0:T(4,128)S(1)} %bitcast.9, bf16[1024,8192]{1,0:T(8,128)(2,1)} %weight.9), custom_call_target="tpu_custom_call" | custom-call | flops 1 | bytes 1 | tf_op jit(solution)/shard_map/gate/pallas_call | solution.py:477
  61.0 0.1 collective-permute-start
  61.1 2.6 %own.2 = f32[176,2048]{1,0:T(8,128)S(1)} custom-call(s32[1]{0:T(128)} %bitcast.place, bf16[176,1024]{1,0:T(8,128)(2,1)S(1)} %get-tuple-element.35.gated.first, bf16[1024,8192]{1,0:T(8,128)(2,1)} %weight.9), custom_call_target="tpu_custom_call" | custom-call | flops 1 | bytes 1 | tf_op jit(solution)/shard_map/own/pallas_call | solution.py:488
  63.7 0.0 collective-permute-done
  63.7 0.2 add_convert_fusion.1
  63.9 1.6 %collective-permute-start.1 = (bf16[176,2048]{1,0:T(8,128)(2,1)S(1)}, bf16[176,2048]{1,0:T(8,128)(2,1)S(1)}, u32[]{:S(2)}, u32[]{:S(2)}) collective-permute-start(bf16[176,2048]{1,0:T(8,128)(2,1)S(1)} %add_convert_fusion.1), channel_id=1, source_target_pairs={{0,2},{1,3},{2,0},{3,1},{4,6},{5,7},{6,4},{7,5},{8,10},{9,11},{10,... | collective-permute-start | bytes 2162696 | tf_op jit(solution)/shard_map/ppermute | solution.py:426
  65.5 11.2 %all_to_all.15.mixed = bf16[8,80,128]{2,1,0:T(8,128)(2,1)S(1)} all-to-all(bf16[8,80,128]{2,1,0:T(8,128)(2,1)S(1)} %get-tuple-element.31), channel_id=1, replica_groups=mesh['seq'=8,'mp'=4] {'seq'}, dimensions={0} | all-to-all | bytes 327680 | tf_op jit(solution)/shard_map/all_to_all | solution.py:429
  76.7 2.6 %gate.3 = (bf16[80,1024]{1,0:T(8,128)(2,1)S(1)}, bf16[80,2048]{1,0:T(8,128)(2,1)S(1)}) custom-call(s32[1]{0:T(128)} %bitcast.place, bf16[8,80,128]{2,1,0:T(8,128)(2,1)S(1)} %all_to_all.15.mixed, bf16[256,1024]{1,0:T(8,128)(2,1)S(1)} %slice_bitcast_fusion.branch, f32[3,3,1024]{2,1,0:T(4,128)S(1)} %bitcast.10, bf16[1024,8192]{1,0:T(8,128)(2,1)} %weight.9), custom_call_target="tpu_custom_call" | custom-call | flops 1 | bytes 1 | tf_op jit(solution)/shard_map/gate/pallas_call | solution.py:477
  79.3 0.1 collective-permute-start.2
  79.4 2.6 %own.3 = f32[80,2048]{1,0:T(8,128)S(1)} custom-call(s32[1]{0:T(128)} %bitcast.place, bf16[80,1024]{1,0:T(8,128)(2,1)S(1)} %get-tuple-element.36.gated.second, bf16[1024,8192]{1,0:T(8,128)(2,1)} %weight.9), custom_call_target="tpu_custom_call" | custom-call | flops 1 | bytes 1 | tf_op jit(solution)/shard_map/own/pallas_call | solution.py:488
  81.9 0.5 collective-permute-done.1
  82.5 0.0 collective-permute-done.2
  82.5 0.1 add_convert_fusion.2
  82.6 1.6 %collective-permute-start.7 = (bf16[80,2048]{1,0:T(8,128)(2,1)S(1)}, bf16[80,2048]{1,0:T(8,128)(2,1)S(1)}, u32[]{:S(2)}, u32[]{:S(2)}) collective-permute-start(bf16[80,2048]{1,0:T(8,128)(2,1)S(1)} %add_convert_fusion.2), channel_id=1, source_target_pairs={{0,2},{1,3},{2,0},{3,1},{4,6},{5,7},{6,4},{7,5},{8,10},{9,11},{10,... | collective-permute-start | bytes 983048 | tf_op jit(solution)/shard_map/ppermute | solution.py:426
  84.1 4.1 %near.1 = (bf16[256,512]{1,0:T(8,128)(2,1)S(1)}, bf16[256,512]{1,0:T(8,128)(2,1)S(1)}, bf16[256,512]{1,0:T(8,128)(2,1)S(1)}, bf16[256,512]{1,0:T(8,128)(2,1)S(1)}, f32[256,2048]{1,0:T(8,128)S(1)}) custom-call(s32[1]{0:T(128)} %bitcast.place, bf16[176,1024]{1,0:T(8,128)(2,1)S(1)} %get-tuple-element.35.gated.first, ...), custom_call_target="tpu_custom_call" | custom-call | flops 1 | bytes 1 | tf_op jit(solution)/shard_map/near/pallas_call | solution.py:506
  88.3 0.1 collective-permute-start.3
  88.3 0.5 collective-permute-start.4
  88.8 0.1 collective-permute-start.5
  88.9 0.4 collective-permute-start.6
  89.4 0.5 collective-permute-done.3
  89.9 0.4 collective-permute-done.4
  90.2 0.4 collective-permute-done.5
  90.6 0.4 collective-permute-done.6
  91.0 1.2 %collective-permute-done.7 = bf16[80,2048]{1,0:T(8,128)(2,1)S(1)} collective-permute-done((bf16[80,2048]{1,0:T(8,128)(2,1)S(1)}, bf16[80,2048]{1,0:T(8,128)(2,1)S(1)}, u32[]{:S(2)}, u32[]{:S(2)}) %collective-permute-start.7) | collective-permute-done | bytes 327712 | tf_op jit(solution)/shard_map/ppermute | solution.py:426
  92.2 1.4 %add_convert_fusion = bf16[256,2048]{1,0:T(8,128)(2,1)} fusion(f32[256,2048]{1,0:T(8,128)S(1)} %get-tuple-element.37, bf16[256,512]{1,0:T(8,128)(2,1)S(1)} %collective-permute-done.6, bf16[256,512]{1,0:T(8,128)(2,1)S(1)} %collective-permute-done.5, bf16[256,512]{1,0:T(8,128)(2,1)S(1)} %collective-permute-done.4, ...), kind=kLoop, calls=%fused_computation | loop fusion | flops 7864320 | bytes 5242880 | tf_op jit(solution)/shard_map/convert_element_type | solution.py:524
  (1 shorter events, 0.0 us)
Async XLA Ops:
  0.0 10.4 %copy-start = (f32[1024]{0:T(1024)S(1)}, f32[1024]{0:T(1024)}, u32[]{:S(2)}) copy-start(f32[1024]{0:T(1024)} %param.10) | copy-start | bytes 12292
  0.0 10.5 %copy-start.1 = (f32[3,1024,3]{1,2,0:T(4,128)S(1)}, f32[3,1024,3]{1,2,0:T(4,128)}, u32[]{:S(2)}) copy-start(f32[3,1024,3]{1,2,0:T(4,128)} %param.8) | copy-start | bytes 110596
  0.0 36.9 %copy-start.2 = (f32[256,32]{1,0:T(8,128)S(1)}, f32[256,32]{1,0:T(8,128)}, u32[]{:S(2)}) copy-start(f32[256,32]{1,0:T(8,128)} %constant.20.clone.twist) | copy-start | bytes 98308
  0.0 36.9 %copy-start.3 = (bf16[512,512]{1,0:T(8,128)(2,1)S(1)}, bf16[512,512]{1,0:T(8,128)(2,1)}, u32[]{:S(2)}) copy-start(bf16[512,512]{1,0:T(8,128)(2,1)} %constant.19.clone.matrix) | copy-start | bytes 1572868
  3.1 33.7 %all-to-all-start = ((bf16[8,528,128]{2,1,0:T(8,128)(2,1)}), bf16[8,528,128]{2,1,0:T(8,128)(2,1)S(1)}, u32[]{:S(2)}, u32[]{:S(2)}) async-start(bf16[8,528,128]{2,1,0:T(8,128)(2,1)} %product.1), calls=%async_computation | async-start | bytes 2162688 | tf_op jit(solution)/shard_map/all_to_all | solution.py:429
  43.6 14.8 %all-to-all-start.1 = ((bf16[8,176,128]{2,1,0:T(8,128)(2,1)}), bf16[8,176,128]{2,1,0:T(8,128)(2,1)S(1)}, u32[]{:S(2)}, u32[]{:S(2)}) async-start(bf16[8,176,128]{2,1,0:T(8,128)(2,1)} %get-tuple-element.27), calls=%async_computation.1 | async-start | bytes 720896 | tf_op jit(solution)/shard_map/all_to_all | solution.py:429
  61.0 2.7 %collective-permute-start = (bf16[176,2048]{1,0:T(8,128)(2,1)S(1)}, bf16[176,2048]{1,0:T(8,128)(2,1)S(1)}, u32[]{:S(2)}, u32[]{:S(2)}) collective-permute-start(bf16[176,2048]{1,0:T(8,128)(2,1)S(1)} %get-tuple-element.30), channel_id=1, source_target_pairs={{0,1},{1,0},{2,3},{3,2},{4,5},{5,4},{6,7},{7,6},{8,9},{9,8},{10,11... | collective-permute-start | bytes 2162696 | tf_op jit(solution)/shard_map/ppermute | solution.py:426
  63.9 18.6 %collective-permute-start.1 = (bf16[176,2048]{1,0:T(8,128)(2,1)S(1)}, bf16[176,2048]{1,0:T(8,128)(2,1)S(1)}, u32[]{:S(2)}, u32[]{:S(2)}) collective-permute-start(bf16[176,2048]{1,0:T(8,128)(2,1)S(1)} %add_convert_fusion.1), channel_id=1, source_target_pairs={{0,2},{1,3},{2,0},{3,1},{4,6},{5,7},{6,4},{7,5},{8,10},{9,11},{10,... | collective-permute-start | bytes 2162696 | tf_op jit(solution)/shard_map/ppermute | solution.py:426
  79.3 3.2 %collective-permute-start.2 = (bf16[80,2048]{1,0:T(8,128)(2,1)S(1)}, bf16[80,2048]{1,0:T(8,128)(2,1)S(1)}, u32[]{:S(2)}, u32[]{:S(2)}) collective-permute-start(bf16[80,2048]{1,0:T(8,128)(2,1)S(1)} %get-tuple-element.34), channel_id=1, source_target_pairs={{0,1},{1,0},{2,3},{3,2},{4,5},{5,4},{6,7},{7,6},{8,9},{9,8},{10,11... | collective-permute-start | bytes 983048 | tf_op jit(solution)/shard_map/ppermute | solution.py:426
  82.6 9.6 %collective-permute-start.7 = (bf16[80,2048]{1,0:T(8,128)(2,1)S(1)}, bf16[80,2048]{1,0:T(8,128)(2,1)S(1)}, u32[]{:S(2)}, u32[]{:S(2)}) collective-permute-start(bf16[80,2048]{1,0:T(8,128)(2,1)S(1)} %add_convert_fusion.2), channel_id=1, source_target_pairs={{0,2},{1,3},{2,0},{3,1},{4,6},{5,7},{6,4},{7,5},{8,10},{9,11},{10,... | collective-permute-start | bytes 983048 | tf_op jit(solution)/shard_map/ppermute | solution.py:426
  88.3 1.6 %collective-permute-start.3 = (bf16[256,512]{1,0:T(8,128)(2,1)S(1)}, bf16[256,512]{1,0:T(8,128)(2,1)S(1)}, u32[]{:S(2)}, u32[]{:S(2)}) collective-permute-start(bf16[256,512]{1,0:T(8,128)(2,1)S(1)} %get-tuple-element.38), channel_id=1, source_target_pairs={{0,1},{1,0},{2,3},{3,2},{4,5},{5,4},{6,7},{7,6},{8,9},{9,8},{10,11... | collective-permute-start | bytes 786440 | tf_op jit(solution)/shard_map/ppermute | solution.py:426
  88.3 1.9 %collective-permute-start.4 = (bf16[256,512]{1,0:T(8,128)(2,1)S(1)}, bf16[256,512]{1,0:T(8,128)(2,1)S(1)}, u32[]{:S(2)}, u32[]{:S(2)}) collective-permute-start(bf16[256,512]{1,0:T(8,128)(2,1)S(1)} %get-tuple-element.39), channel_id=1, source_target_pairs={{0,1},{1,0},{2,3},{3,2},{4,5},{5,4},{6,7},{7,6},{8,9},{9,8},{10,11... | collective-permute-start | bytes 786440 | tf_op jit(solution)/shard_map/ppermute | solution.py:426
  88.8 1.8 %collective-permute-start.5 = (bf16[256,512]{1,0:T(8,128)(2,1)S(1)}, bf16[256,512]{1,0:T(8,128)(2,1)S(1)}, u32[]{:S(2)}, u32[]{:S(2)}) collective-permute-start(bf16[256,512]{1,0:T(8,128)(2,1)S(1)} %get-tuple-element.40), channel_id=1, source_target_pairs={{0,1},{1,0},{2,3},{3,2},{4,5},{5,4},{6,7},{7,6},{8,9},{9,8},{10,11... | collective-permute-start | bytes 786440 | tf_op jit(solution)/shard_map/ppermute | solution.py:426
  88.9 2.1 %collective-permute-start.6 = (bf16[256,512]{1,0:T(8,128)(2,1)S(1)}, bf16[256,512]{1,0:T(8,128)(2,1)S(1)}, u32[]{:S(2)}, u32[]{:S(2)}) collective-permute-start(bf16[256,512]{1,0:T(8,128)(2,1)S(1)} %get-tuple-element.41), channel_id=1, source_target_pairs={{0,1},{1,0},{2,3},{3,2},{4,5},{5,4},{6,7},{7,6},{8,9},{9,8},{10,11... | collective-permute-start | bytes 786440 | tf_op jit(solution)/shard_map/ppermute | solution.py:426

commit v5 on v4

--- a/solution.py
+++ b/solution.py
@@ -97,7 +97,7 @@
 VMEM = pl.BlockSpec(memory_space=pltpu.VMEM)
 SMEM = pl.BlockSpec(memory_space=pltpu.SMEM)
 HBM = pl.BlockSpec(memory_space=pltpu.HBM)
-TILE = 512
+TILE = 256
 PIECES = 4
 STEPS = 4
 BRANCHES = 3

time: 94 us -> 94 us (level)
  no operation moved by 1% of the time
where the time goes in v5:
time: 94 us; the launch traced here: 93.6 us
  waiting for transfers between devices  39.9 us (42%)
  Pallas kernels  24.3 us (26%)
  starting transfers between devices  15.3 us (16%)
  blocking collectives  11.2 us (12%)
  other arithmetic  1.63 us (2%)
  local copies, waits for them, and re-layouts  1.17 us (1%)
    all_to_all x2, waiting for transfers between devices, across(): return lax.all_to_all(value, 'seq', 0, 0, tiled=True)  36.5 us
    all_to_all x1, blocking collectives, across(): return lax.all_to_all(value, 'seq', 0, 0, tiled=True)  11.2 us
    all_to_all x2, starting transfers between devices, across(): return lax.all_to_all(value, 'seq', 0, 0, tiled=True)  10.9 us
    pallas_call x2, Pallas kernels, shards(): pl.pallas_call(functools.partial(gate_kernel, start), in_specs=[SMEM] + [...  5.2 us
    pallas_call x2, Pallas kernels, shards(): pl.pallas_call(own_kernel, in_specs=[SMEM, VMEM, HBM], out_specs=VMEM, ou...  5.18 us
    pallas_call x1, Pallas kernels, shards(): pl.pallas_call(transform_kernel, in_specs=[VMEM] * 4, out_specs=[VMEM] *...  4.63 us
    ppermute x8, starting transfers between devices, exchanged(): return lax.ppermute(value, 'mp', [(m, m ^ bit) for m in range(mp_count)])  4.4 us
    pallas_call x1, Pallas kernels, shards(): pl.pallas_call(near_kernel, in_specs=[SMEM, VMEM, VMEM, HBM], out_specs=[...  4.13 us
  transfers between devices with their start and end apart: 10, of which 8 were waited for; matrix products, arithmetic and copies ran while one was open for 1% of the time, Pallas kernels for 13%

profile of v5, /device:TPU:0, one launch (start us, length us, event | category | flops | bytes accessed | tf_op | source)
XLA Modules:
  0.0 93.6 jit_solution(5111509989820006171)
XLA Ops:
  0.0 0.0 copy-start
  0.0 0.0 copy-start.1
  0.0 0.0 copy-start.2
  0.0 0.0 copy-start.3
  0.0 3.1 %product.1 = bf16[8,528,128]{2,1,0:T(8,128)(2,1)} custom-call(f32[3,3,1024]{2,1,0:T(4,128)} %bitcast.8, bf16[3,256,1024]{2,1,0:T(8,128)(2,1)} %branches.1, bf16[256,1024]{1,0:T(8,128)(2,1)} %filt.1), custom_call_target="tpu_custom_call" | custom-call | flops 10485760 | bytes 2621440 | tf_op jit(solution)/shard_map/product/pallas_call | solution.py:179
  3.1 7.3 %all-to-all-start = ((bf16[8,528,128]{2,1,0:T(8,128)(2,1)}), bf16[8,528,128]{2,1,0:T(8,128)(2,1)S(1)}, u32[]{:S(2)}, u32[]{:S(2)}) async-start(bf16[8,528,128]{2,1,0:T(8,128)(2,1)} %product.1), calls=%async_computation | async-start | bytes 2162688 | tf_op jit(solution)/shard_map/all_to_all | solution.py:429
  10.4 0.0 copy-done
  10.4 0.1 dynamic-slice_bitcast_fusion.1.gain
  10.5 0.0 copy-done.1
  10.5 26.4 %all-to-all-done.signals = bf16[8,528,128]{2,1,0:T(8,128)(2,1)S(1)} async-done(((bf16[8,528,128]{2,1,0:T(8,128)(2,1)}), bf16[8,528,128]{2,1,0:T(8,128)(2,1)S(1)}, u32[]{:S(2)}, u32[]{:S(2)}) %all-to-all-start) | async-done | bytes 1081376 | tf_op jit(solution)/shard_map/all_to_all | solution.py:429
  36.9 0.0 copy-done.2
  36.9 0.0 copy-done.3
  36.9 4.6 %transform.1 = (f32[5,512,256]{2,1,0:T(8,128)S(1)}, bf16[8,256,128]{2,1,0:T(8,128)(2,1)S(1)}, f32[8,16,128]{2,1,0:T(8,128)S(1)}) custom-call(bf16[512,512]{1,0:T(8,128)(2,1)S(1)} %copy-done.3, f32[256,32]{1,0:T(8,128)S(1)} %copy-done.2, f32[3,3,128]{2,1,0:T(4,128)S(1)} %dynamic-slice_bitcast_fusion.taps, bf16[8,528,128]{2,1,0:T(8,128)(2,1)S(1)} %all-to-all-done.signals), custom_call_target="tpu_custom_call" | custom-call | flops 3221225472 | bytes 6291456 | tf_op jit(solution)/shard_map/transform/pallas_call | solution.py:441
  41.5 2.1 %back.1 = (bf16[8,176,128]{2,1,0:T(8,128)(2,1)}, bf16[8,80,128]{2,1,0:T(8,128)(2,1)S(1)}) custom-call(f32[256,32]{1,0:T(8,128)S(1)} %copy-done.2, f32[1,128]{1,0:T(1,128)S(1)} %dynamic-slice_bitcast_fusion.1.gain, f32[8,16,128]{2,1,0:T(8,128)S(1)} %get-tuple-element.24.gates, f32[5,512,256]{2,1,0:T(8,128)S(1)} %get-tuple-element.25.turned, ...), custom_call_target="tpu_custom_call" | custom-call | flops 52428800 | bytes 5242880 | tf_op jit(solution)/shard_map/back/pallas_call | solution.py:456
  43.6 3.6 %all-to-all-start.1 = ((bf16[8,176,128]{2,1,0:T(8,128)(2,1)}), bf16[8,176,128]{2,1,0:T(8,128)(2,1)S(1)}, u32[]{:S(2)}, u32[]{:S(2)}) async-start(bf16[8,176,128]{2,1,0:T(8,128)(2,1)} %get-tuple-element.27), calls=%async_computation.1 | async-start | bytes 720896 | tf_op jit(solution)/shard_map/all_to_all | solution.py:429
  47.2 1.1 %slice_bitcast_fusion.branch = bf16[256,1024]{1,0:T(8,128)(2,1)S(1)} fusion(bf16[3,256,1024]{2,1,0:T(8,128)(2,1)} %branches.1), kind=kLoop, calls=%fused_computation.3 | loop fusion | bytes 1048576 | tf_op jit(solution)/shard_map/squeeze | solution.py:486
  48.3 10.1 %all-to-all-done.1.mixed = bf16[8,176,128]{2,1,0:T(8,128)(2,1)S(1)} async-done(((bf16[8,176,128]{2,1,0:T(8,128)(2,1)}), bf16[8,176,128]{2,1,0:T(8,128)(2,1)S(1)}, u32[]{:S(2)}, u32[]{:S(2)}) %all-to-all-start.1) | async-done | bytes 360480 | tf_op jit(solution)/shard_map/all_to_all | solution.py:429
  58.4 2.6 %gate.2 = (bf16[176,1024]{1,0:T(8,128)(2,1)S(1)}, bf16[176,2048]{1,0:T(8,128)(2,1)S(1)}) custom-call(s32[1]{0:T(128)} %bitcast.place, bf16[8,176,128]{2,1,0:T(8,128)(2,1)S(1)} %all-to-all-done.1.mixed, bf16[256,1024]{1,0:T(8,128)(2,1)S(1)} %slice_bitcast_fusion.branch, f32[3,3,1024]{2,1,0:T(4,128)S(1)} %bitcast.9, bf16[1024,8192]{1,0:T(8,128)(2,1)} %weight.9), custom_call_target="tpu_custom_call" | custom-call | flops 1 | bytes 1 | tf_op jit(solution)/shard_map/gate/pallas_call | solution.py:477
  61.0 0.1 collective-permute-start
  61.1 2.6 %own.2 = f32[176,2048]{1,0:T(8,128)S(1)} custom-call(s32[1]{0:T(128)} %bitcast.place, bf16[176,1024]{1,0:T(8,128)(2,1)S(1)} %get-tuple-element.35.gated.first, bf16[1024,8192]{1,0:T(8,128)(2,1)} %weight.9), custom_call_target="tpu_custom_call" | custom-call | flops 1 | bytes 1 | tf_op jit(solution)/shard_map/own/pallas_call | solution.py:488
  63.7 0.0 collective-permute-done
  63.7 0.2 add_convert_fusion.1
  63.9 1.6 %collective-permute-start.1 = (bf16[176,2048]{1,0:T(8,128)(2,1)S(1)}, bf16[176,2048]{1,0:T(8,128)(2,1)S(1)}, u32[]{:S(2)}, u32[]{:S(2)}) collective-permute-start(bf16[176,2048]{1,0:T(8,128)(2,1)S(1)} %add_convert_fusion.1), channel_id=1, source_target_pairs={{0,2},{1,3},{2,0},{3,1},{4,6},{5,7},{6,4},{7,5},{8,10},{9,11},{10,... | collective-permute-start | bytes 2162696 | tf_op jit(solution)/shard_map/ppermute | solution.py:426
  65.5 11.2 %all_to_all.15.mixed = bf16[8,80,128]{2,1,0:T(8,128)(2,1)S(1)} all-to-all(bf16[8,80,128]{2,1,0:T(8,128)(2,1)S(1)} %get-tuple-element.31), channel_id=1, replica_groups=mesh['seq'=8,'mp'=4] {'seq'}, dimensions={0} | all-to-all | bytes 327680 | tf_op jit(solution)/shard_map/all_to_all | solution.py:429
  76.7 2.6 %gate.3 = (bf16[80,1024]{1,0:T(8,128)(2,1)S(1)}, bf16[80,2048]{1,0:T(8,128)(2,1)S(1)}) custom-call(s32[1]{0:T(128)} %bitcast.place, bf16[8,80,128]{2,1,0:T(8,128)(2,1)S(1)} %all_to_all.15.mixed, bf16[256,1024]{1,0:T(8,128)(2,1)S(1)} %slice_bitcast_fusion.branch, f32[3,3,1024]{2,1,0:T(4,128)S(1)} %bitcast.10, bf16[1024,8192]{1,0:T(8,128)(2,1)} %weight.9), custom_call_target="tpu_custom_call" | custom-call | flops 1 | bytes 1 | tf_op jit(solution)/shard_map/gate/pallas_call | solution.py:477
  79.3 0.1 collective-permute-start.2
  79.4 2.6 %own.3 = f32[80,2048]{1,0:T(8,128)S(1)} custom-call(s32[1]{0:T(128)} %bitcast.place, bf16[80,1024]{1,0:T(8,128)(2,1)S(1)} %get-tuple-element.36.gated.second, bf16[1024,8192]{1,0:T(8,128)(2,1)} %weight.9), custom_call_target="tpu_custom_call" | custom-call | flops 1 | bytes 1 | tf_op jit(solution)/shard_map/own/pallas_call | solution.py:488
  81.9 0.5 collective-permute-done.1
  82.5 0.0 collective-permute-done.2
  82.5 0.1 add_convert_fusion.2
  82.6 1.6 %collective-permute-start.7 = (bf16[80,2048]{1,0:T(8,128)(2,1)S(1)}, bf16[80,2048]{1,0:T(8,128)(2,1)S(1)}, u32[]{:S(2)}, u32[]{:S(2)}) collective-permute-start(bf16[80,2048]{1,0:T(8,128)(2,1)S(1)} %add_convert_fusion.2), channel_id=1, source_target_pairs={{0,2},{1,3},{2,0},{3,1},{4,6},{5,7},{6,4},{7,5},{8,10},{9,11},{10,... | collective-permute-start | bytes 983048 | tf_op jit(solution)/shard_map/ppermute | solution.py:426
  84.1 4.1 %near.1 = (bf16[256,512]{1,0:T(8,128)(2,1)S(1)}, bf16[256,512]{1,0:T(8,128)(2,1)S(1)}, bf16[256,512]{1,0:T(8,128)(2,1)S(1)}, bf16[256,512]{1,0:T(8,128)(2,1)S(1)}, f32[256,2048]{1,0:T(8,128)S(1)}) custom-call(s32[1]{0:T(128)} %bitcast.place, bf16[176,1024]{1,0:T(8,128)(2,1)S(1)} %get-tuple-element.35.gated.first, ...), custom_call_target="tpu_custom_call" | custom-call | flops 1 | bytes 1 | tf_op jit(solution)/shard_map/near/pallas_call | solution.py:506
  88.3 0.1 collective-permute-start.3
  88.3 0.5 collective-permute-start.4
  88.8 0.1 collective-permute-start.5
  88.9 0.4 collective-permute-start.6
  89.4 0.5 collective-permute-done.3
  89.9 0.4 collective-permute-done.4
  90.2 0.4 collective-permute-done.5
  90.6 0.4 collective-permute-done.6
  91.0 1.2 %collective-permute-done.7 = bf16[80,2048]{1,0:T(8,128)(2,1)S(1)} collective-permute-done((bf16[80,2048]{1,0:T(8,128)(2,1)S(1)}, bf16[80,2048]{1,0:T(8,128)(2,1)S(1)}, u32[]{:S(2)}, u32[]{:S(2)}) %collective-permute-start.7) | collective-permute-done | bytes 327712 | tf_op jit(solution)/shard_map/ppermute | solution.py:426
  92.2 1.4 %add_convert_fusion = bf16[256,2048]{1,0:T(8,128)(2,1)} fusion(f32[256,2048]{1,0:T(8,128)S(1)} %get-tuple-element.37, bf16[256,512]{1,0:T(8,128)(2,1)S(1)} %collective-permute-done.6, bf16[256,512]{1,0:T(8,128)(2,1)S(1)} %collective-permute-done.5, bf16[256,512]{1,0:T(8,128)(2,1)S(1)} %collective-permute-done.4, ...), kind=kLoop, calls=%fused_computation | loop fusion | flops 7864320 | bytes 5242880 | tf_op jit(solution)/shard_map/convert_element_type | solution.py:524
  (1 shorter events, 0.0 us)
Async XLA Ops:
  0.0 10.4 %copy-start = (f32[1024]{0:T(1024)S(1)}, f32[1024]{0:T(1024)}, u32[]{:S(2)}) copy-start(f32[1024]{0:T(1024)} %param.10) | copy-start | bytes 12292
  0.0 10.5 %copy-start.1 = (f32[3,1024,3]{1,2,0:T(4,128)S(1)}, f32[3,1024,3]{1,2,0:T(4,128)}, u32[]{:S(2)}) copy-start(f32[3,1024,3]{1,2,0:T(4,128)} %param.8) | copy-start | bytes 110596
  0.0 36.9 %copy-start.2 = (f32[256,32]{1,0:T(8,128)S(1)}, f32[256,32]{1,0:T(8,128)}, u32[]{:S(2)}) copy-start(f32[256,32]{1,0:T(8,128)} %constant.20.clone.twist) | copy-start | bytes 98308
  0.0 36.9 %copy-start.3 = (bf16[512,512]{1,0:T(8,128)(2,1)S(1)}, bf16[512,512]{1,0:T(8,128)(2,1)}, u32[]{:S(2)}) copy-start(bf16[512,512]{1,0:T(8,128)(2,1)} %constant.19.clone.matrix) | copy-start | bytes 1572868
  3.1 33.7 %all-to-all-start = ((bf16[8,528,128]{2,1,0:T(8,128)(2,1)}), bf16[8,528,128]{2,1,0:T(8,128)(2,1)S(1)}, u32[]{:S(2)}, u32[]{:S(2)}) async-start(bf16[8,528,128]{2,1,0:T(8,128)(2,1)} %product.1), calls=%async_computation | async-start | bytes 2162688 | tf_op jit(solution)/shard_map/all_to_all | solution.py:429
  43.6 14.8 %all-to-all-start.1 = ((bf16[8,176,128]{2,1,0:T(8,128)(2,1)}), bf16[8,176,128]{2,1,0:T(8,128)(2,1)S(1)}, u32[]{:S(2)}, u32[]{:S(2)}) async-start(bf16[8,176,128]{2,1,0:T(8,128)(2,1)} %get-tuple-element.27), calls=%async_computation.1 | async-start | bytes 720896 | tf_op jit(solution)/shard_map/all_to_all | solution.py:429
  61.0 2.7 %collective-permute-start = (bf16[176,2048]{1,0:T(8,128)(2,1)S(1)}, bf16[176,2048]{1,0:T(8,128)(2,1)S(1)}, u32[]{:S(2)}, u32[]{:S(2)}) collective-permute-start(bf16[176,2048]{1,0:T(8,128)(2,1)S(1)} %get-tuple-element.30), channel_id=1, source_target_pairs={{0,1},{1,0},{2,3},{3,2},{4,5},{5,4},{6,7},{7,6},{8,9},{9,8},{10,11... | collective-permute-start | bytes 2162696 | tf_op jit(solution)/shard_map/ppermute | solution.py:426
  63.9 18.6 %collective-permute-start.1 = (bf16[176,2048]{1,0:T(8,128)(2,1)S(1)}, bf16[176,2048]{1,0:T(8,128)(2,1)S(1)}, u32[]{:S(2)}, u32[]{:S(2)}) collective-permute-start(bf16[176,2048]{1,0:T(8,128)(2,1)S(1)} %add_convert_fusion.1), channel_id=1, source_target_pairs={{0,2},{1,3},{2,0},{3,1},{4,6},{5,7},{6,4},{7,5},{8,10},{9,11},{10,... | collective-permute-start | bytes 2162696 | tf_op jit(solution)/shard_map/ppermute | solution.py:426
  79.3 3.2 %collective-permute-start.2 = (bf16[80,2048]{1,0:T(8,128)(2,1)S(1)}, bf16[80,2048]{1,0:T(8,128)(2,1)S(1)}, u32[]{:S(2)}, u32[]{:S(2)}) collective-permute-start(bf16[80,2048]{1,0:T(8,128)(2,1)S(1)} %get-tuple-element.34), channel_id=1, source_target_pairs={{0,1},{1,0},{2,3},{3,2},{4,5},{5,4},{6,7},{7,6},{8,9},{9,8},{10,11... | collective-permute-start | bytes 983048 | tf_op jit(solution)/shard_map/ppermute | solution.py:426
  82.6 9.6 %collective-permute-start.7 = (bf16[80,2048]{1,0:T(8,128)(2,1)S(1)}, bf16[80,2048]{1,0:T(8,128)(2,1)S(1)}, u32[]{:S(2)}, u32[]{:S(2)}) collective-permute-start(bf16[80,2048]{1,0:T(8,128)(2,1)S(1)} %add_convert_fusion.2), channel_id=1, source_target_pairs={{0,2},{1,3},{2,0},{3,1},{4,6},{5,7},{6,4},{7,5},{8,10},{9,11},{10,... | collective-permute-start | bytes 983048 | tf_op jit(solution)/shard_map/ppermute | solution.py:426
  88.3 1.6 %collective-permute-start.3 = (bf16[256,512]{1,0:T(8,128)(2,1)S(1)}, bf16[256,512]{1,0:T(8,128)(2,1)S(1)}, u32[]{:S(2)}, u32[]{:S(2)}) collective-permute-start(bf16[256,512]{1,0:T(8,128)(2,1)S(1)} %get-tuple-element.38), channel_id=1, source_target_pairs={{0,1},{1,0},{2,3},{3,2},{4,5},{5,4},{6,7},{7,6},{8,9},{9,8},{10,11... | collective-permute-start | bytes 786440 | tf_op jit(solution)/shard_map/ppermute | solution.py:426
  88.3 1.9 %collective-permute-start.4 = (bf16[256,512]{1,0:T(8,128)(2,1)S(1)}, bf16[256,512]{1,0:T(8,128)(2,1)S(1)}, u32[]{:S(2)}, u32[]{:S(2)}) collective-permute-start(bf16[256,512]{1,0:T(8,128)(2,1)S(1)} %get-tuple-element.39), channel_id=1, source_target_pairs={{0,1},{1,0},{2,3},{3,2},{4,5},{5,4},{6,7},{7,6},{8,9},{9,8},{10,11... | collective-permute-start | bytes 786440 | tf_op jit(solution)/shard_map/ppermute | solution.py:426
  88.8 1.8 %collective-permute-start.5 = (bf16[256,512]{1,0:T(8,128)(2,1)S(1)}, bf16[256,512]{1,0:T(8,128)(2,1)S(1)}, u32[]{:S(2)}, u32[]{:S(2)}) collective-permute-start(bf16[256,512]{1,0:T(8,128)(2,1)S(1)} %get-tuple-element.40), channel_id=1, source_target_pairs={{0,1},{1,0},{2,3},{3,2},{4,5},{5,4},{6,7},{7,6},{8,9},{9,8},{10,11... | collective-permute-start | bytes 786440 | tf_op jit(solution)/shard_map/ppermute | solution.py:426
  88.9 2.1 %collective-permute-start.6 = (bf16[256,512]{1,0:T(8,128)(2,1)S(1)}, bf16[256,512]{1,0:T(8,128)(2,1)S(1)}, u32[]{:S(2)}, u32[]{:S(2)}) collective-permute-start(bf16[256,512]{1,0:T(8,128)(2,1)S(1)} %get-tuple-element.41), channel_id=1, source_target_pairs={{0,1},{1,0},{2,3},{3,2},{4,5},{5,4},{6,7},{7,6},{8,9},{9,8},{10,11... | collective-permute-start | bytes 786440 | tf_op jit(solution)/shard_map/ppermute | solution.py:426
